TPU v7x, 512 devices: a whole 4x8x8 slice. The times are simulated.
512 devices in a mesh: gx: 32 (over x_hi, z, core), gy: 16 (over y, x_lo).
Axes of the slice: x: 4 (x_hi: 2, x_lo: 2; x = x_hi * 2 + x_lo), y: 8, z: 8, core: 2. Of those that a mesh axis runs over, the one named last changes fastest.
Arguments:
- coords: float32 [32, 16, 3, 1024], P('gx', 'gy'), may hold values from 0 to 1
- multipoles: float32 [32, 16, 10, 1024], P('gx', 'gy'), may hold values from -3 to 3
- face_atoms: int32 [32, 16, 3, 512], P('gx', 'gy'), may hold values from 0 to 1023, as said below
- tile_pairs: int32 [32, 16, 2, 32], P('gx', 'gy'), may hold values from 0 to 19, as said below
- tile_count: int32 [32, 16], P('gx', 'gy'), may hold values from 16 to 32
- frame_atoms: int32 [32, 16, 3, 1024], P('gx', 'gy'), may hold values from 0 to 2559, as said below
- send_list: int32 [32, 16, 3, 128], P('gx', 'gy'), may hold values from 0 to 511, as said below
- send_count: int32 [32, 16, 3], P('gx', 'gy'), may hold values from 42 to 128
Outputs:
- forces: float32 [32, 16, 3, 1024], P('gx', 'gy')
Inputs may be any that keep to these rules, and one draw needn't show every extreme that they name: `face_atoms`: within one set of one domain the 512 atoms are distinct. `tile_pairs`: row 0 is below 8, row 1 is at least row 0; the tiles of one domain are distinct pairs of blocks; every block of imported atoms is the row 1 block of some live tile. `frame_atoms`: A frame atom differs from its own atom; a frame atom in an imported set is one of the live entries of that set's send list, and every live entry of a send list is the frame atom of some owned atom. `send_list`: the 128 entries of one list are distinct.
All inputs are finite; a program needn't handle non-finite values.
Results may differ from a plain program's by a relative error of at most 0.0003.
Values sent between devices are 32-bit elements; how exact they have to be, the bound alone decides.
A program may use at most 64 MiB of HBM per device.

v0:
```python
import jax
import jax.numpy as jnp
from jax import lax
from jax.sharding import PartitionSpec as P

SOFTENING = 0.5
LEVER_SOFT = 0.04
tile_group = 2


def from_behind(array, axis, by):
    peers = lax.axis_size(axis)
    return lax.ppermute(array, axis, [(i, (i + by) % peers) for i in range(peers)])


def cross_product(lhs_vec, rhs_vec):
    return (
        lhs_vec[1] * rhs_vec[2] - lhs_vec[2] * rhs_vec[1],
        lhs_vec[2] * rhs_vec[0] - lhs_vec[0] * rhs_vec[2],
        lhs_vec[0] * rhs_vec[1] - lhs_vec[1] * rhs_vec[0],
    )


def inner_product(lhs_vec, rhs_vec):
    return lhs_vec[0] * rhs_vec[0] + lhs_vec[1] * rhs_vec[1] + lhs_vec[2] * rhs_vec[2]


def quad_matrix(entries):
    return (
        (entries[0], entries[3], entries[4]),
        (entries[3], entries[1], entries[5]),
        (entries[4], entries[5], entries[2]),
    )


def apply_matrix(matrix, vector):
    return tuple(
        (
            matrix[row_id][0] * vector[0]
            + matrix[row_id][1] * vector[1]
            + matrix[row_id][2] * vector[2]
            for row_id in range(3)
        )
    )


def pair_energy(place_near, place_far, moment_near, moment_far, weight):
    between = tuple((place_far[row_id] - place_near[row_id] for row_id in range(3)))
    distance_sq = inner_product(between, between) + SOFTENING
    radial = [lax.rsqrt(distance_sq)]
    for order_id in range(4):
        radial.append((2 * order_id + 1) * radial[order_id] / distance_sq)
    charge_near = moment_near[0]
    charge_far = moment_far[0]
    dipole_near = (moment_near[1], moment_near[2], moment_near[3])
    dipole_far = (moment_far[1], moment_far[2], moment_far[3])
    quadrupole_near = quad_matrix(moment_near[4:10])
    quadrupole_far = quad_matrix(moment_far[4:10])
    turned_near = apply_matrix(quadrupole_near, between)
    turned_far = apply_matrix(quadrupole_far, between)
    along_near = inner_product(dipole_near, between)
    along_far = inner_product(dipole_far, between)
    double_near = inner_product(between, turned_near)
    double_far = inner_product(between, turned_far)
    quad_both = jnp.zeros_like(distance_sq)
    for row_id in range(3):
        for column_id in range(3):
            quad_both = (
                quad_both + quadrupole_near[row_id][column_id] * quadrupole_far[row_id][column_id]
            )
    energy = charge_near * charge_far * radial[0]
    energy = (
        energy
        + (
            charge_far * along_near
            - charge_near * along_far
            + inner_product(dipole_near, dipole_far)
        )
        * radial[1]
    )
    energy = (
        energy
        + (
            charge_near * double_far
            + charge_far * double_near
            - along_near * along_far
            + 2.0
            * (
                inner_product(dipole_far, turned_near)
                - inner_product(dipole_near, turned_far)
                + quad_both
            )
        )
        * radial[2]
    )
    energy = (
        energy
        + (
            along_near * double_far
            - along_far * double_near
            - 4.0 * inner_product(turned_near, turned_far)
        )
        * radial[3]
    )
    energy = energy + double_near * double_far * radial[4]
    return jnp.sum(energy * weight)


def torque_from(moment, slope):
    from_dipole = cross_product((moment[1], moment[2], moment[3]), (slope[1], slope[2], slope[3]))
    quadrupole = quad_matrix(moment[4:10])
    quad_slope = quad_matrix(
        (slope[4], slope[5], slope[6], 0.5 * slope[7], 0.5 * slope[8], 0.5 * slope[9])
    )

    def commutator(row_id, column_id):
        summed = (
            quadrupole[row_id][0] * quad_slope[0][column_id]
            - quad_slope[row_id][0] * quadrupole[0][column_id]
        )
        for inner_id in (1, 2):
            summed = (
                summed
                + quadrupole[row_id][inner_id] * quad_slope[inner_id][column_id]
                - quad_slope[row_id][inner_id] * quadrupole[inner_id][column_id]
            )
        return summed

    return jnp.stack(
        [
            2.0 * commutator(2, 1) - from_dipole[0],
            2.0 * commutator(0, 2) - from_dipole[1],
            2.0 * commutator(1, 0) - from_dipole[2],
        ]
    )


def tile_terms(near_block, far_block, weight):
    slopes = jax.grad(pair_energy, argnums=(0, 1, 2, 3))(
        near_block[0:3, :, None],
        far_block[0:3, None, :],
        near_block[3:13, :, None],
        far_block[3:13, None, :],
        weight,
    )
    return (
        -slopes[0][:, :, 0],
        torque_from(near_block[3:13], slopes[2][:, :, 0]),
        -slopes[1][:, 0, :],
        torque_from(far_block[3:13], slopes[3][:, 0, :]),
    )


def group_terms(pooled, blocks_near, blocks_far, alive):
    lanes = jnp.arange(128, dtype=jnp.int32)
    rows_near = blocks_near[:, None] * 128 + lanes[None, :]
    rows_far = blocks_far[:, None] * 128 + lanes[None, :]
    near_block = jnp.take(pooled, rows_near, axis=1)
    far_block = jnp.take(pooled, rows_far, axis=1)
    upper_half = lanes[:, None] < lanes[None, :]
    keep_pair = alive[:, None, None] & (
        (blocks_near != blocks_far)[:, None, None] | upper_half[None]
    )
    weight = jnp.where(keep_pair, 1.0, 0.0).astype(pooled.dtype)
    force_near, torque_near, force_far, torque_far = jax.vmap(tile_terms, in_axes=(1, 1, 0))(
        near_block, far_block, weight
    )
    values = jnp.concatenate(
        [
            jnp.concatenate([force_near, torque_near], axis=1),
            jnp.concatenate([force_far, torque_far], axis=1),
        ],
        axis=0,
    )
    values = jnp.transpose(values, (1, 0, 2)).reshape(6, -1)
    targets = jnp.concatenate([rows_near, rows_far], axis=0).reshape(-1)
    return (targets, values)


def device_pairs(pooled, tile_rows, live_tiles, group_count):

    def accumulate(group_id, partials):
        offset_row = group_id.astype(jnp.int32) * tile_group
        blocks_near = lax.dynamic_slice_in_dim(tile_rows[0], offset_row, tile_group)
        blocks_far = lax.dynamic_slice_in_dim(tile_rows[1], offset_row, tile_group)
        alive = offset_row + jnp.arange(tile_group, dtype=jnp.int32) < live_tiles
        targets, values = group_terms(pooled, blocks_near, blocks_far, alive)
        return partials.at[:, targets].add(values)

    return lax.fori_loop(0, group_count, accumulate, jnp.zeros((6, pooled.shape[1]), pooled.dtype))


def frame_section(pool_place, torque, frames):
    own_count = frames.shape[1]
    own_place = pool_place[:, :own_count]
    frame_place = jnp.take(pool_place, frames, axis=1)
    lever = frame_place - own_place[:, None, :]
    scale = 1.0 / (3.0 * (inner_product(lever, lever) + LEVER_SOFT))
    push = jnp.stack(cross_product(torque[:, None, :], lever)) * scale[None]
    spread = (
        jnp.zeros(pool_place.shape, pool_place.dtype)
        .at[:, frames.reshape(-1)]
        .add(push.reshape(3, -1))
    )
    return spread.at[:, :own_count].add(-jnp.sum(push, axis=1))


def masked_set(halo_values, chosen, live_count):
    alive = (jnp.arange(chosen.shape[0], dtype=jnp.int32) < live_count).astype(halo_values.dtype)
    keep_mask = jnp.zeros((halo_values.shape[1],), halo_values.dtype).at[chosen].add(alive)
    return halo_values * keep_mask[None, :]


def shards(
    coords, multipoles, face_atoms, tile_pairs, tile_count, frame_atoms, send_list, send_count
):
    stacked = jnp.concatenate([coords[0, 0], multipoles[0, 0]], axis=0)
    face_rows = face_atoms[0, 0]
    own_count = stacked.shape[1]
    halo_count = face_rows.shape[1]
    exports = jnp.take(stacked, face_rows, axis=1)
    unit_x = jnp.zeros((13, 1), jnp.float32).at[0, 0].set(1.0)
    unit_y = jnp.zeros((13, 1), jnp.float32).at[1, 0].set(1.0)
    import_x = from_behind(exports[:, 0], "gx", -1) + unit_x
    import_y = from_behind(exports[:, 1], "gy", -1) + unit_y
    relayed = from_behind(exports[:, 2], "gx", -1)
    import_c = from_behind(relayed, "gy", -1)
    import_c = import_c + unit_x + unit_y
    pooled = jnp.concatenate([stacked, import_x, import_y, import_c], axis=1)
    live_tiles = tile_count[0, 0]
    partials = device_pairs(
        pooled, tile_pairs[0, 0], live_tiles, (live_tiles + tile_group - 1) // tile_group
    )
    halo_back = partials[:, own_count:].reshape(6, 3, halo_count)
    return_x = from_behind(halo_back[:, 0], "gx", 1)
    return_y = from_behind(halo_back[:, 1], "gy", 1)
    relayed_back = from_behind(halo_back[:, 2], "gx", 1)
    return_c = from_behind(relayed_back, "gy", 1)
    owned = (
        partials[:, :own_count]
        .at[:, face_rows[0]]
        .add(return_x)
        .at[:, face_rows[1]]
        .add(return_y)
        .at[:, face_rows[2]]
        .add(return_c)
    )
    spread = frame_section(pooled[0:3], owned[3:6], frame_atoms[0, 0])
    forces = owned[0:3] + spread[:, :own_count]
    spread_halo = spread[:, own_count:].reshape(3, 3, halo_count)
    chosen = send_list[0, 0]
    counts = send_count[0, 0]
    dense_x = from_behind(masked_set(spread_halo[:, 0], chosen[0], counts[0]), "gx", 1)
    dense_y = from_behind(masked_set(spread_halo[:, 1], chosen[1], counts[1]), "gy", 1)
    dense_relay = from_behind(masked_set(spread_halo[:, 2], chosen[2], counts[2]), "gx", 1)
    dense_c = from_behind(dense_relay, "gy", 1)
    forces = (
        forces.at[:, face_rows[0]]
        .add(dense_x)
        .at[:, face_rows[1]]
        .add(dense_y)
        .at[:, face_rows[2]]
        .add(dense_c)
    )
    return forces[None, None]


def solution(mesh):
    placed = (
        P("gx", "gy", None, None),
        P("gx", "gy", None, None),
        P("gx", "gy", None, None),
        P("gx", "gy", None, None),
        P("gx", "gy"),
        P("gx", "gy", None, None),
        P("gx", "gy", None, None),
        P("gx", "gy", None),
    )
    return jax.shard_map(
        shards, mesh=mesh, in_specs=placed, out_specs=P("gx", "gy", None, None), check_vma=False
    )
```

profile of v0, /device:TPU:6, one launch (start us, length us, event | category | flops | bytes accessed | tf_op | source)
XLA Modules:
  0.0 430.6 jit_solution(1295915483194649779)
XLA Ops:
  3.3 2.6 gather_fusion.2
  6.2 11.2 %collective-permute-start = (f32[13,512]{1,0:T(8,128)S(1)}, f32[13,512]{1,0:T(8,128)S(1)}, u32[]{:S(2)}, u32[]{:S(2)}) collective-permute-start(f32[13,512]{1,0:T(8,128)S(1)} %get-tuple-element.222), channel_id=1, source_target_pairs={{0,496},{16,0},{32,16},{48,32},{64,48},{80,64},{96,80},{112,96},{1... | collective-permute-start | bytes 79880 | tf_op jit(solution)/shard_map/ppermute | solution.py:13
  17.4 2.6 collective-permute-start.2
  20.0 1.9 collective-permute-start.1
  23.4 6.8 %collective-permute-start.3 = (f32[13,512]{1,0:T(8,128)S(1)}, f32[13,512]{1,0:T(8,128)S(1)}, u32[]{:S(2)}, u32[]{:S(2)}) collective-permute-start(f32[13,512]{1,0:T(8,128)S(1)} %collective-permute-done.2), channel_id=1, source_target_pairs={{0,15},{1,0},{2,1},{3,2},{4,3},{5,4},{6,5},{7,6},{8,7},{9,8},{10,9... | collective-permute-start | bytes 79880 | tf_op jit(solution)/shard_map/ppermute | solution.py:13
  32.6 226.5 %while.13 = (s32[]{:T(128)}, f32[6,2560]{0,1:T(8,128)S(1)}, s32[]{:T(128)}, s32[2,32]{1,0:T(2,128)S(1)}, f32[13,2560]{0,1:T(8,128)S(1)}, /*index=5*/s32[]{:T(128)}, s32[]{:T(128)}, s32[]{:T(128)}, s32[]{:T(128)}, s32[]{:T(128)}) while((s32[]{:T(128)}, f32[6,2560]{0,1:T(8,128)S(1)}, s32[]{:T(128)}, s32[2,32]{1,0:T(2,128)S(1)}, ...), condition=%wide.region_62.64_spmd, body=%wide.region_0.63_spmd.sunk | while | flops 50423824 | bytes 1341247 | solution.py:190
  38.8 1.6 fusion.231
  47.6 3.8 scatter_fusion
  66.5 3.8 scatter_fusion
  76.5 1.6 fusion.231
  85.4 3.8 scatter_fusion
  95.4 1.6 fusion.231
  104.2 3.8 scatter_fusion
  123.1 3.8 scatter_fusion
  133.2 1.6 fusion.231
  142.0 3.8 scatter_fusion
  152.0 1.6 fusion.231
  160.9 3.8 scatter_fusion
  170.9 1.6 fusion.231
  179.8 3.8 scatter_fusion
  198.6 3.8 scatter_fusion
  208.7 1.6 fusion.231
  217.5 3.8 scatter_fusion
  227.5 1.6 fusion.231
  236.4 3.8 scatter_fusion
  246.4 1.6 fusion.231
  255.3 3.8 scatter_fusion
  259.9 76.6 %collective-permute-start.6 = (f32[6,512]{0,1:T(8,128)}, f32[6,512]{0,1:T(8,128)}, u32[]{:S(2)}, u32[]{:S(2)}) collective-permute-start(f32[6,512]{0,1:T(8,128)} %get-tuple-element.219), channel_id=1, source_target_pairs={{0,16},{16,32},{32,48},{48,64},{64,80},{80,96},{96,112},{112,128},... | collective-permute-start | bytes 36872 | tf_op jit(solution)/shard_map/ppermute | solution.py:13
  342.5 10.8 %gather_fusion.3 = f32[3072,3]{1,0:T(8,128)} fusion(f32[3,2560]{0,1:T(8,128)S(1)} %copy.135, s32[3072]{0:T(1024)S(1)} %broadcast_clamp_fusion), kind=kCustom, calls=%fused_computation.3 | custom fusion | bytes 86016 | tf_op jit(solution)/shard_map/jit(_take)/gather | solution.py:196
  353.4 2.0 copy.136
  355.4 1.9 collective-permute-start.4
  357.3 1.9 collective-permute-start.5
  359.3 1.9 collective-permute-start.7
  361.3 5.4 %collective-permute-done.4 = f32[6,512]{0,1:T(8,128)S(1)} collective-permute-done((f32[6,512]{0,1:T(8,128)S(1)}, f32[6,512]{0,1:T(8,128)S(1)}, u32[]{:S(2)}, u32[]{:S(2)}) %collective-permute-start.4) | collective-permute-done | bytes 12320 | tf_op jit(solution)/shard_map/ppermute | solution.py:13
  366.7 3.5 scatter_custom_fusion.1
  370.2 3.5 scatter_custom_fusion.2
  373.8 3.7 scatter_custom_fusion.3
  378.6 1.7 copy.137
  380.3 17.6 %scatter_custom_fusion.4 = f32[3,2560]{0,1:T(8,128)S(1)} fusion(s32[3072]{0:T(1024)S(1)} %bitcast.661, f32[3072,3]{1,0:T(8,128)} %copy.137, f32[]{:T(128)} %constant.193.clone.1), kind=kCustom, calls=%fused_computation.431 | custom fusion | flops 9216 | bytes 31232 | tf_op jit(solution)/shard_map/scatter-add | solution.py:203
  398.9 1.9 collective-permute-start.10
  401.1 1.9 collective-permute-start.8
  403.1 2.4 collective-permute-start.9
  405.5 7.7 %collective-permute-done.10 = f32[3,512]{0,1:T(8,128)} collective-permute-done((f32[3,512]{0,1:T(8,128)S(1)}, f32[3,512]{0,1:T(8,128)}, u32[]{:S(2)}, u32[]{:S(2)}) %collective-permute-start.10) | collective-permute-done | bytes 6176 | tf_op jit(solution)/shard_map/ppermute | solution.py:13
  413.2 1.9 collective-permute-start.11
  415.8 3.0 collective-permute-done.8
  418.8 3.9 scatter_custom_fusion.6
  422.7 3.5 scatter_custom_fusion.8
  426.2 3.5 scatter_custom_fusion.10
  (1094 shorter events, 178.3 us)
Async XLA Ops:
  2.9 19.0 %copy-start = (s32[1,1,3,1024]{3,1,2,0:T(1,128)S(1)}, s32[1,1,3,1024]{3,1,2,0:T(1,128)}, u32[]{:S(2)}) copy-start(s32[1,1,3,1024]{3,1,2,0:T(1,128)} %param.23) | copy-start | bytes 36868
  3.2 18.8 %copy-start.1 = (s32[1,1,3,512]{3,1,2,0:T(1,128)S(1)}, s32[1,1,3,512]{3,1,2,0:T(1,128)}, u32[]{:S(2)}) copy-start(s32[1,1,3,512]{3,1,2,0:T(1,128)} %param.20) | copy-start | bytes 18436
  3.2 18.9 %copy-start.4 = (s32[1,1,3,128]{3,1,2,0:T(1,128)S(1)}, s32[1,1,3,128]{3,1,2,0:T(1,128)}, u32[]{:S(2)}) copy-start(s32[1,1,3,128]{3,1,2,0:T(1,128)} %param.24) | copy-start | bytes 4612
  3.2 18.9 %copy-start.3 = (s32[1,1,3]{2,1,0:T(1,128)S(1)}, s32[1,1,3]{2,1,0:T(1,128)}, u32[]{:S(2)}) copy-start(s32[1,1,3]{2,1,0:T(1,128)} %param.25) | copy-start | bytes 40
  3.2 28.5 %copy-start.5 = (f32[13]{0:T(128)S(1)}, f32[13]{0:T(128)}, u32[]{:S(2)}) copy-start(f32[13]{0:T(128)} %constant.199.clone.1) | copy-start | bytes 160
  3.2 28.5 %copy-start.6 = (f32[13]{0:T(128)S(1)}, f32[13]{0:T(128)}, u32[]{:S(2)}) copy-start(f32[13]{0:T(128)} %constant.200.clone.1) | copy-start | bytes 160
  6.2 25.2 %collective-permute-start = (f32[13,512]{1,0:T(8,128)S(1)}, f32[13,512]{1,0:T(8,128)S(1)}, u32[]{:S(2)}, u32[]{:S(2)}) collective-permute-start(f32[13,512]{1,0:T(8,128)S(1)} %get-tuple-element.222), channel_id=1, source_target_pairs={{0,496},{16,0},{32,16},{48,32},{64,48},{80,64},{96,80},{112,96},{1... | collective-permute-start | bytes 79880 | tf_op jit(solution)/shard_map/ppermute | solution.py:13
  17.4 5.9 %collective-permute-start.2 = (f32[13,512]{1,0:T(8,128)S(1)}, f32[13,512]{1,0:T(8,128)S(1)}, u32[]{:S(2)}, u32[]{:S(2)}) collective-permute-start(f32[13,512]{1,0:T(8,128)S(1)} %get-tuple-element.223), channel_id=1, source_target_pairs={{0,496},{16,0},{32,16},{48,32},{64,48},{80,64},{96,80},{112,96},{1... | collective-permute-start | bytes 79880 | tf_op jit(solution)/shard_map/ppermute | solution.py:13
  20.0 11.4 %collective-permute-start.1 = (f32[13,512]{1,0:T(8,128)S(1)}, f32[13,512]{1,0:T(8,128)S(1)}, u32[]{:S(2)}, u32[]{:S(2)}) collective-permute-start(f32[13,512]{1,0:T(8,128)S(1)} %get-tuple-element.224), channel_id=1, source_target_pairs={{0,15},{1,0},{2,1},{3,2},{4,3},{5,4},{6,5},{7,6},{8,7},{9,8},{10,9... | collective-permute-start | bytes 79880 | tf_op jit(solution)/shard_map/ppermute | solution.py:13
  23.4 8.4 %collective-permute-start.3 = (f32[13,512]{1,0:T(8,128)S(1)}, f32[13,512]{1,0:T(8,128)S(1)}, u32[]{:S(2)}, u32[]{:S(2)}) collective-permute-start(f32[13,512]{1,0:T(8,128)S(1)} %collective-permute-done.2), channel_id=1, source_target_pairs={{0,15},{1,0},{2,1},{3,2},{4,3},{5,4},{6,5},{7,6},{8,7},{9,8},{10,9... | collective-permute-start | bytes 79880 | tf_op jit(solution)/shard_map/ppermute | solution.py:13
  31.9 0.7 copy-start.2
  259.9 99.4 %collective-permute-start.6 = (f32[6,512]{0,1:T(8,128)}, f32[6,512]{0,1:T(8,128)}, u32[]{:S(2)}, u32[]{:S(2)}) collective-permute-start(f32[6,512]{0,1:T(8,128)} %get-tuple-element.219), channel_id=1, source_target_pairs={{0,16},{16,32},{32,48},{48,64},{64,80},{80,96},{96,112},{112,128},... | collective-permute-start | bytes 36872 | tf_op jit(solution)/shard_map/ppermute | solution.py:13
  355.4 11.3 %collective-permute-start.4 = (f32[6,512]{0,1:T(8,128)S(1)}, f32[6,512]{0,1:T(8,128)S(1)}, u32[]{:S(2)}, u32[]{:S(2)}) collective-permute-start(f32[6,512]{0,1:T(8,128)S(1)} %get-tuple-element.221), channel_id=1, source_target_pairs={{0,16},{16,32},{32,48},{48,64},{64,80},{80,96},{96,112},{112,128},... | collective-permute-start | bytes 36872 | tf_op jit(solution)/shard_map/ppermute | solution.py:13
  357.3 12.9 %collective-permute-start.5 = (f32[6,512]{0,1:T(8,128)S(1)}, f32[6,512]{0,1:T(8,128)S(1)}, u32[]{:S(2)}, u32[]{:S(2)}) collective-permute-start(f32[6,512]{0,1:T(8,128)S(1)} %get-tuple-element.220), channel_id=1, source_target_pairs={{0,1},{1,2},{2,3},{3,4},{4,5},{5,6},{6,7},{7,8},{8,9},{9,10},{10,1... | collective-permute-start | bytes 36872 | tf_op jit(solution)/shard_map/ppermute | solution.py:13
  359.3 14.5 %collective-permute-start.7 = (f32[6,512]{0,1:T(8,128)}, f32[6,512]{0,1:T(8,128)S(1)}, u32[]{:S(2)}, u32[]{:S(2)}) collective-permute-start(f32[6,512]{0,1:T(8,128)} %collective-permute-done.6), channel_id=1, source_target_pairs={{0,1},{1,2},{2,3},{3,4},{4,5},{5,6},{6,7},{7,8},{8,9},{9,10},{10,1... | collective-permute-start | bytes 36872 | tf_op jit(solution)/shard_map/ppermute | solution.py:13
  398.9 14.2 %collective-permute-start.10 = (f32[3,512]{0,1:T(8,128)S(1)}, f32[3,512]{0,1:T(8,128)}, u32[]{:S(2)}, u32[]{:S(2)}) collective-permute-start(f32[3,512]{0,1:T(8,128)S(1)} %get-tuple-element.216), channel_id=1, source_target_pairs={{0,16},{16,32},{32,48},{48,64},{64,80},{80,96},{96,112},{112,128},... | collective-permute-start | bytes 18440 | tf_op jit(solution)/shard_map/ppermute | solution.py:13
  401.1 17.6 %collective-permute-start.8 = (f32[3,512]{0,1:T(8,128)}, f32[3,512]{0,1:T(8,128)}, u32[]{:S(2)}, u32[]{:S(2)}) collective-permute-start(f32[3,512]{0,1:T(8,128)} %get-tuple-element.218), channel_id=1, source_target_pairs={{0,16},{16,32},{32,48},{48,64},{64,80},{80,96},{96,112},{112,128},... | collective-permute-start | bytes 18440 | tf_op jit(solution)/shard_map/ppermute | solution.py:13
  403.1 19.6 %collective-permute-start.9 = (f32[3,512]{0,1:T(8,128)}, f32[3,512]{0,1:T(8,128)S(1)}, u32[]{:S(2)}, u32[]{:S(2)}) collective-permute-start(f32[3,512]{0,1:T(8,128)} %get-tuple-element.217), channel_id=1, source_target_pairs={{0,1},{1,2},{2,3},{3,4},{4,5},{5,6},{6,7},{7,8},{8,9},{9,10},{10,1... | collective-permute-start | bytes 18440 | tf_op jit(solution)/shard_map/ppermute | solution.py:13
  413.2 13.1 %collective-permute-start.11 = (f32[3,512]{0,1:T(8,128)}, f32[3,512]{0,1:T(8,128)S(1)}, u32[]{:S(2)}, u32[]{:S(2)}) collective-permute-start(f32[3,512]{0,1:T(8,128)} %collective-permute-done.10), channel_id=1, source_target_pairs={{0,1},{1,2},{2,3},{3,4},{4,5},{5,6},{6,7},{7,8},{8,9},{9,10},{10,1... | collective-permute-start | bytes 18440 | tf_op jit(solution)/shard_map/ppermute | solution.py:13
where the time goes:
time: 431 us
  other arithmetic  249 us (58%)
  starting transfers between devices  113 us (26%)
  local copies, waits for them, and re-layouts  45.3 us (11%)
  waiting for transfers between devices  16.4 us (4%)
  loops' own time  5.61 us (1%)
    ppermute x12, starting transfers between devices, from_behind(): lax.ppermute(array, axis, [(i, (i + by) % peers) for i in range(peers)])  113 us
    reduce_sum x36, other arithmetic, pair_energy(): place_far[row_id] - place_near[row_id]  57.7 us
    scatter-add x12, other arithmetic, accumulate(): return partials.at[:, targets].add(values)  45.4 us
    reduce_sum x48, other arithmetic, apply_matrix(): matrix[row_id][2] * vector[2]  25.7 us
    scatter-add x1, other arithmetic, frame_section(): spread = jnp.zeros(pool_place.shape, pool_place.dtype).at[:, frames.resha...  17.6 us
    ppermute x12, waiting for transfers between devices, from_behind(): lax.ppermute(array, axis, [(i, (i + by) % peers) for i in range(peers)])  16.4 us
    reduce_sum x36, other arithmetic, apply_matrix(): matrix[row_id][1] * vector[1]  16.3 us
    reduce_sum x36, other arithmetic, apply_matrix(): matrix[row_id][0] * vector[0] + matrix[row_id][1] * vector[1]  16.1 us
  transfers between devices with their start and end apart: 12, of which 4 were waited for; matrix products, arithmetic and copies ran while one was open for 8% of the time, Pallas kernels for 0%

commit v1 on v0

v1 whole, which is shorter than its diff:
```python
import jax
import jax.numpy as jnp
from jax import lax
from jax.experimental import pallas as pl
from jax.experimental.pallas import tpu as pltpu
from jax.sharding import PartitionSpec as P

SOFTENING = 0.5
LEVER_SOFT = 0.04
OWN_BLOCKS = 8
POOL_BLOCKS = 20
ROWS = 24
ENTRIES = ((0, 0), (1, 1), (2, 2), (0, 1), (0, 2), (1, 2))
ENTRY_AT = {(0, 0): 0, (1, 1): 1, (2, 2): 2, (0, 1): 3, (1, 0): 3, (0, 2): 4, (2, 0): 4, (1, 2): 5, (2, 1): 5}
MULT = (1.0, 1.0, 1.0, 2.0, 2.0, 2.0)
F32 = jnp.float32
BF16 = jnp.bfloat16
ACC_GROUPS = 18
MESH = pl.DeviceIdType.MESH


def cross3(a, b):
    return (a[1] * b[2] - a[2] * b[1], a[2] * b[0] - a[0] * b[2], a[0] * b[1] - a[1] * b[0])


def dot3(a, b):
    return a[0] * b[0] + a[1] * b[1] + a[2] * b[2]


def mat_vec(m, v):
    return [sum_list([m[ENTRY_AT[(r, c)]] * v[c] for c in range(3)]) for r in range(3)]


def sum_list(items):
    total = items[0]
    for item in items[1:]:
        total = total + item
    return total


def sym_outer(a, b):
    out = []
    for r, c in ENTRIES:
        if r == c:
            out.append(a[r] * b[r])
        else:
            out.append(0.5 * (a[r] * b[c] + a[c] * b[r]))
    return out


def split2(value):
    hi = value.astype(BF16).astype(F32)
    lo = (value - hi).astype(BF16).astype(F32)
    return hi, lo


def nt_dot(a, b):
    return lax.dot_general(a, b, (((1,), (1,)), ((), ())), preferred_element_type=F32)


def mm(a, b):
    return lax.dot_general(a, b, (((1,), (0,)), ((), ())), preferred_element_type=F32)


def lane_gather(row, index):
    table = jnp.broadcast_to(row, (8, 128))
    return jnp.take_along_axis(table, index, axis=1)


def face_masks(face_rows):
    sub8 = lax.broadcasted_iota(jnp.int32, (8, 128), 0)
    sub128 = lax.broadcasted_iota(jnp.int32, (128, 128), 0)
    blocks, lanes = [], []
    for row in face_rows:
        blocks.append(jnp.broadcast_to(row >> 7, (8, 128)) == sub8)
        hit = jnp.broadcast_to(row & 127, (128, 128)) == sub128
        lanes.append(jnp.where(hit, 1.0, 0.0).astype(BF16))
    return blocks, lanes


def scatter_faces(values, blocks, lanes):
    comps = len(values)
    columns = []
    for j in range(len(blocks)):
        parts = []
        for c in range(comps):
            hi, lo = split2(values[c][j])
            parts.append(jnp.where(blocks[j], jnp.broadcast_to(hi, (8, 128)), 0.0))
            parts.append(jnp.where(blocks[j], jnp.broadcast_to(lo, (8, 128)), 0.0))
        columns.append(jnp.concatenate(parts, axis=0).astype(BF16))
    lhs = jnp.concatenate(columns, axis=1)
    rhs = jnp.concatenate(lanes, axis=1)
    out = nt_dot(lhs, rhs)
    return [out[16 * c : 16 * c + 8] + out[16 * c + 8 : 16 * c + 16] for c in range(comps)]


def export_body(coords_ref, mult_ref, face_ref, own_ref, out_ref):
    for c in range(13):
        src, row = (coords_ref, c) if c < 3 else (mult_ref, c - 3)
        for b in range(OWN_BLOCKS):
            own_ref[c, b : b + 1, :] = src[0, 0, row : row + 1, b * 128 : (b + 1) * 128]
    face = jnp.concatenate(
        [face_ref[0, 0, k : k + 1, j * 128 : (j + 1) * 128] for k in range(3) for j in range(4)]
        + [jnp.zeros((4, 128), jnp.int32)],
        axis=0,
    )
    shift = lax.broadcasted_iota(jnp.int32, (16, 128), 0)
    shift_x = jnp.where((shift < 4) | (shift >= 8), 1.0, 0.0).astype(F32)
    shift_y = jnp.where(shift >= 4, 1.0, 0.0).astype(F32)
    halves = [face[0:8], face[8:16]]
    lows = [h & 127 for h in halves]
    highs = [h >> 7 for h in halves]
    for c in range(13):
        got = []
        for part in range(2):
            total = jnp.zeros((8, 128), F32)
            for b in range(OWN_BLOCKS):
                picked = lane_gather(own_ref[c, b : b + 1, :], lows[part])
                total = jnp.where(highs[part] == b, picked, total)
            got.append(total)
        rows = jnp.concatenate(got, axis=0)
        if c == 0:
            rows = rows + shift_x
        if c == 1:
            rows = rows + shift_y
        for k in range(3):
            out_ref[k, 4 * c : 4 * c + 4, :] = rows[4 * k : 4 * k + 4]


def exchange_body(step, sizes, send_ref, recv_ref, send_sem, recv_sem):
    gx, gy = lax.axis_index("gx"), lax.axis_index("gy")
    nx, ny = sizes
    up = (lax.rem(gx + 1, nx), lax.rem(gy + 1, ny))
    down = (lax.rem(gx + nx - 1, nx), lax.rem(gy + ny - 1, ny))
    to = up if step > 0 else down
    barrier = pltpu.get_barrier_semaphore()
    for other in (up, down):
        for peer in ((other[0], gy), (gx, other[1]), (other[0], other[1])):
            pl.semaphore_signal(barrier, inc=1, device_id=peer, device_id_type=MESH)
    pl.semaphore_wait(barrier, 6)
    copies = []
    for k, peer in enumerate(((to[0], gy), (gx, to[1]), (to[0], to[1]))):
        copy = pltpu.make_async_remote_copy(
            src_ref=send_ref.at[k],
            dst_ref=recv_ref.at[k],
            send_sem=send_sem.at[k],
            recv_sem=recv_sem.at[k],
            device_id=peer,
            device_id_type=MESH,
        )
        copy.start()
        copies.append(copy)
    for copy in copies:
        copy.wait()


def pool_features(pool):
    x = [pool[0] - 1.0, pool[1] - 1.0, pool[2] - 0.5]
    q = pool[3]
    d = [pool[4], pool[5], pool[6]]
    quad = [pool[7], pool[8], pool[9], pool[10], pool[11], pool[12]]
    one = jnp.ones_like(q)
    xx = [x[r] * x[c] for r, c in ENTRIES]
    qx = [q * x[r] for r in range(3)]
    m = [qx[r] + d[r] for r in range(3)]
    turned = mat_vec(quad, x)
    dx = dot3(d, x)
    xqx = dot3(x, turned)
    sdx = sym_outer(d, x)
    h = [q * xx[e] + 2.0 * sdx[e] for e in range(6)]
    tx = sym_outer(turned, x)
    outer = [[quad[e] * x[c] for c in range(3)] for e in range(6)]
    return dict(one=one, x=x, q=q, d=d, quad=quad, xx=xx, qx=qx, m=m, turned=turned, dx=dx, xqx=xqx, h=h, tx=tx, outer=outer)


def sum_rows(f):
    zero = jnp.zeros_like(f["one"])
    rows = [f["one"], *f["x"], f["q"], *f["d"]]
    rows += [*f["qx"], *f["m"], zero, zero]
    rows += [*f["quad"], *f["turned"], *f["h"], zero]
    rows += [*f["tx"]] + [f["outer"][e][c] for e in range(6) for c in range(3)]
    rows += [*f["xx"], zero, zero]
    return rows


def near_rows(f):
    zero = jnp.zeros_like(f["one"])
    first = [*f["d"], f["dx"], *f["quad"], *f["turned"], f["xqx"], f["one"], *f["x"], *f["xx"]]
    second = [*f["d"], f["dx"], f["q"], *f["qx"], *f["quad"], *f["turned"], f["xqx"], *f["h"]]
    third = [*f["quad"], *f["turned"], *f["tx"]] + [f["outer"][e][c] for e in range(6) for c in range(3)]
    return first + second + third + [zero] * 7


def far_rows(f):
    zero = jnp.zeros_like(f["one"])
    one = f["one"]
    x, d, q, xx = f["x"], f["d"], f["q"], f["xx"]
    quad, turned = f["quad"], f["turned"]
    z = lambda n: [zero] * n
    u = [3.0 * x[r] for r in range(3)] + [-3.0 * one] + z(20)
    v = z(14) + [3.0 * f["dx"]] + [-3.0 * d[r] for r in range(3)] + z(6)
    p = z(4) + [15.0 * MULT[e] * xx[e] for e in range(6)] + [-30.0 * x[r] for r in range(3)] + [15.0 * one] + z(10)
    r_ = (
        z(14)
        + [15.0 * f["xqx"]]
        + [-30.0 * turned[r] for r in range(3)]
        + [15.0 * MULT[e] * quad[e] for e in range(6)]
    )
    l1 = [1.8 * f["m"][r] for r in range(3)] + [-1.8 * q, -1.8 * f["dx"]] + [1.8 * d[r] for r in range(3)]
    l1 += z(16)
    l2 = (
        [-18.0 * turned[r] for r in range(3)]
        + z(1)
        + [9.0 * f["xqx"]]
        + [-18.0 * turned[r] for r in range(3)]
        + [9.0 * MULT[e] * (f["h"][e] + 2.0 * quad[e]) for e in range(6)]
        + [-18.0 * f["m"][r] for r in range(3)]
        + [9.0 * q]
        + [9.0 * MULT[e] * quad[e] for e in range(6)]
    )
    l3 = [-180.0 * MULT[e] * f["tx"][e] for e in range(6)] + [180.0 * turned[r] for r in range(3)]
    l3 += [-180.0 * MULT[e] * quad[e] for e in range(6)]
    for a, b in ENTRIES:
        for c in range(3):
            term = quad[ENTRY_AT[(a, c)]] * x[b]
            if a != b:
                term = term + quad[ENTRY_AT[(b, c)]] * x[a]
            l3.append(180.0 * term)
    l3 += z(7)
    return [u, v, p, r_, l1, l2, l3]


def tile_setup(pool_ref, sum_scr, near_scr, far_scr, feat_ref, lhs_ref, rhs_ref, place_ref, wide_ref):
    f = pool_features([pool_ref[c] for c in range(13)])
    for n, row in enumerate(sum_rows(f)):
        sum_scr[n * ROWS : (n + 1) * ROWS, :] = row
    for n, row in enumerate(near_rows(f)):
        near_scr[n * 8 : n * 8 + 8, :] = row[0:8]
    at = 0
    for group in far_rows(f):
        for row in group:
            far_scr[at * ROWS : (at + 1) * ROWS, :] = row
            at += 1

    def per_block(b, _):
        sums = sum_scr[pl.ds(b, 64, stride=ROWS), :]
        place_ref[b] = sums[0:8]
        hi, lo = split2(sums)
        parts = []
        for g in range(8):
            parts += [hi[8 * g : 8 * g + 8], lo[8 * g : 8 * g + 8]]
        feat_ref[b] = jnp.concatenate(parts, axis=0).astype(BF16)
        start = 0
        for out_id, count in enumerate((24, 24, 24, 24, 24, 24, 40)):
            rows = far_scr[pl.ds(b + start * ROWS, count, stride=ROWS), :]
            start += count
            hi, lo = split2(rows)
            pad = [jnp.zeros((128 - 3 * count, 128), F32)]
            stacked = jnp.concatenate([hi, lo, hi] + pad, axis=0).astype(BF16)
            rhs_ref[b, :, out_id * 128 : (out_id + 1) * 128] = stacked
        return 0

    lax.fori_loop(0, POOL_BLOCKS, per_block, 0)

    def per_near(b, _):
        start = 0
        for group, count in enumerate((24, 24, 40)):
            rows = near_scr[pl.ds(b + start * 8, count, stride=8), :]
            start += count
            hi, lo = split2(rows)
            stacked = jnp.concatenate([hi, hi, lo, jnp.zeros((128 - 3 * count, 128), F32)], axis=0)
            lhs_ref[b, :, group * 128 : (group + 1) * 128] = stacked.T.astype(BF16)
        place = jnp.concatenate([place_ref[b], jnp.zeros((120, 128), F32)], axis=0).T
        for r in range(3):
            wide_ref[b, r] = jnp.broadcast_to(place[:, r + 1 : r + 2], (128, 128))
        return 0

    lax.fori_loop(0, OWN_BLOCKS, per_near, 0)


def tile_work(near, far, feat_ref, lhs_ref, rhs_ref, place_ref, wide_ref, keep_ref, keep):
    first = mm(lhs_ref[near, :, 0:128], rhs_ref[far, :, 0:512])
    second = mm(lhs_ref[near, :, 128:256], rhs_ref[far, :, 512:768])
    third = mm(lhs_ref[near, :, 256:384], rhs_ref[far, :, 768:896])
    chunk = 32
    names = ("b1", "b2", "b3", "al", "be", "ga", "de", "e1")
    pieces = {name: ([], []) for name in names}
    place = [jnp.broadcast_to(place_ref[far, r + 1 : r + 2, :], (chunk, 128)) for r in range(3)]
    for row in range(0, 128, chunk):
        rows = slice(row, row + chunk)
        diff = [place[r] - wide_ref[near, r, rows, :] for r in range(3)]
        dist = diff[0] * diff[0] + (diff[1] * diff[1] + (diff[2] * diff[2] + SOFTENING))
        root = lax.rsqrt(dist)
        t = root * root
        b0 = root * keep_ref[keep, rows, :]
        b1 = b0 * t
        b2 = b1 * t
        b3 = b2 * t
        b4 = b3 * (1.4 * t)
        b5 = b4 * (1.8 * t)
        u, v = first[rows, 0:128], first[rows, 128:256]
        p, r_ = first[rows, 256:384], first[rows, 384:512]
        l1, l2, l3 = second[rows, 0:128], second[rows, 128:256], third[rows, :]
        al = r_ * b3 - v * b2
        be = p * b3 + u * b2
        ga = r_ * b4 - v * b3
        de = p * b4 + u * b3
        e1 = l1 * b2 + (l2 - u * v) * b3 + (u * r_ - v * p + l3) * b4 + (p * r_) * b5
        for name, value in zip(names, (b1, b2, b3, al, be, ga, de, e1)):
            hi = value.astype(BF16)
            pieces[name][0].append(hi)
            pieces[name][1].append((value - hi.astype(F32)).astype(BF16))
    return {name: (jnp.concatenate(h, axis=0), jnp.concatenate(l, axis=0)) for name, (h, l) in pieces.items()}


def tile_sums(w, near, far, feat_ref, add):
    near_pairs = (
        ("al", "be", 16, ((0, 0),), ((1, 0),)),
        ("e1", "b1", 32, ((2, 0),), ((3, 0), (4, 1))),
        ("b2", "de", 64, ((5, 0), (6, 1), (7, 2), (8, 3)), ((9, 2), (10, 3))),
        ("ga", "b3", 128, ((11, 0), (12, 7)), ((13, 2), (14, 3), (15, 4), (16, 5), (17, 6))),
    )
    far_pairs = (
        ("be", "al", 16, ((0, 0),), ((1, 0),)),
        ("e1", "b1", 32, ((2, 0),), ((3, 0), (4, 1))),
        ("b2", "ga", 64, ((5, 0), (6, 1), (7, 2), (8, 3)), ((9, 2), (10, 3))),
        ("de", "b3", 128, ((11, 0), (12, 7)), ((13, 2), (14, 3), (15, 4), (16, 5), (17, 6))),
    )
    for pairs, source, target, transposed in ((near_pairs, far, near, True), (far_pairs, near, far, False)):
        for one, two, rows, slots_one, slots_two in pairs:
            feats = feat_ref[source, 0:rows, :]
            lhs = jnp.concatenate([feats, feats], axis=1)
            if transposed:
                rhs = jnp.concatenate(
                    [jnp.concatenate(w[one], axis=1), jnp.concatenate(w[two], axis=1)], axis=0
                )
                out = nt_dot(lhs, rhs)
            else:
                rhs = jnp.concatenate(
                    [jnp.concatenate([w[one][s], w[two][s]], axis=1) for s in range(2)], axis=0
                )
                out = mm(lhs, rhs)
            for half, slots in enumerate((slots_one, slots_two)):
                lanes = slice(128 * half, 128 * half + 128)
                for slot, group in slots:
                    at = 16 * group
                    add(target, slot, out[at : at + 8, lanes] + out[at + 8 : at + 16, lanes])


def finish_sums(load, f):
    x, q, d, quad = f["x"], f["q"], f["d"], f["quad"]
    turned = f["turned"]
    a_one, a_x = load(0, 0), [load(0, 1 + r) for r in range(3)]
    ap_d = [load(1, 5 + r) for r in range(3)]
    e_one, e_x = load(2, 0), [load(2, 1 + r) for r in range(3)]
    b1_q, b1_d = load(3, 4), [load(3, 5 + r) for r in range(3)]
    b1_qx = [load(4, r) for r in range(3)]
    b2_q, b2_m = load(5, 4), [load(6, 3 + r) for r in range(3)]

    def wide(slot):
        flat = lambda n: load(slot + n // 8, n % 8)
        return [flat(e) for e in range(6)], [flat(6 + r) for r in range(3)]

    b2_quad, b2_t = wide(7)
    b2_h = [load(7 + (9 + e) // 8, (9 + e) % 8) for e in range(6)]
    cp_quad, cp_t = wide(9)
    c_one, c_x = load(11, 0), [load(11, 1 + r) for r in range(3)]
    c_xx = [load(12, e) for e in range(6)]
    b3_quad, b3_t = wide(13)
    b3_tx = [load(15, e) for e in range(6)]
    b3_outer = [[load(15 + (6 + 3 * e + c) // 8, (6 + 3 * e + c) % 8) for c in range(3)] for e in range(6)]

    b2_quad_x = mat_vec(b2_quad, x)
    b3_quad_x = mat_vec(b3_quad, x)
    cp_quad_x = mat_vec(cp_quad, x)
    b2_turn = [b2_t[r] - b2_quad_x[r] for r in range(3)]
    b3_turn = [b3_t[r] - b3_quad_x[r] for r in range(3)]
    cp_turn = [cp_t[r] - cp_quad_x[r] for r in range(3)]
    b1_r = [b1_qx[r] - x[r] * b1_q for r in range(3)]
    a_r = [a_x[r] - x[r] * a_one for r in range(3)]
    e_r = [e_x[r] - x[r] * e_one for r in range(3)]
    c_r = [c_x[r] - x[r] * c_one for r in range(3)]
    b2_r = [b2_m[r] - x[r] * b2_q for r in range(3)]

    slope_d = [a_r[r] + b1_r[r] + b1_d[r] - 6.0 * b2_turn[r] for r in range(3)]

    sx_c = sym_outer(c_x, x)
    sx_m = sym_outer(b2_m, x)
    sx_t = sym_outer(b3_t, x)
    sx_q = sym_outer(b3_quad_x, x)
    mixed = [
        [sum_list([b3_outer[ENTRY_AT[(a, c)]][b] * x[c] for c in range(3)]) for b in range(3)] for a in range(3)
    ]
    slope_q = []
    for e, (a, b) in enumerate(ENTRIES):
        ym = mixed[a][b] if a == b else 0.5 * (mixed[a][b] + mixed[b][a])
        slope_q.append(
            5.0 * (c_xx[e] - 2.0 * sx_c[e] + c_one * f["xx"][e])
            + 3.0 * (b2_h[e] - 2.0 * sx_m[e] + b2_q * f["xx"][e])
            + 6.0 * b2_quad[e]
            - 60.0 * (b3_tx[e] - sx_t[e] - ym + sx_q[e])
        )

    inner = [10.0 * c_r[r] + 6.0 * b2_r[r] - 60.0 * b3_turn[r] for r in range(3)]
    inner = mat_vec(quad, inner)
    b2_quad_d = mat_vec(b2_quad, d)
    b3_quad_t = mat_vec(b3_quad, turned)
    force = []
    for a in range(3):
        spun = sum_list(
            [
                b3_outer[ENTRY_AT[(a, b)]][c] * quad[ENTRY_AT[(b, c)]]
                for b in range(3)
                for c in range(3)
            ]
        )
        force.append(
            -q * (b1_r[a] + b1_d[a])
            - (5.0 / 3.0) * e_r[a]
            + d[a] * (a_one + b1_q)
            - ap_d[a]
            + inner[a]
            + 10.0 * cp_turn[a]
            + 6.0 * q * b2_turn[a]
            - 6.0 * b2_quad_d[a]
            - 60.0 * (spun - b3_quad_t[a])
        )

    full = lambda m, r, c: m[ENTRY_AT[(r, c)]]

    def commutator(r, c):
        return sum_list(
            [full(quad, r, k) * full(slope_q, k, c) - full(slope_q, r, k) * full(quad, k, c) for k in range(3)]
        )

    twist = cross3(d, slope_d)
    torque = [
        2.0 * commutator(2, 1) - twist[0],
        2.0 * commutator(0, 2) - twist[1],
        2.0 * commutator(1, 0) - twist[2],
    ]
    return force, torque


def tiles_body(
    own_ref, import_ref, pairs_ref, count_ref, own_out, halo_out,
    pool_ref, sum_scr, near_scr, far_scr, feat_ref, lhs_ref, rhs_ref, place_ref, wide_ref, keep_ref, acc_ref,
):
    for c in range(13):
        pool_ref[c, 0:8, :] = own_ref[c]
        for k in range(3):
            pool_ref[c, 8 + 4 * k : 12 + 4 * k, :] = import_ref[k, 4 * c : 4 * c + 4, :]
        pool_ref[c, 20:24, :] = jnp.zeros((4, 128), F32)
    above = lax.broadcasted_iota(jnp.int32, (128, 128), 0) < lax.broadcasted_iota(jnp.int32, (128, 128), 1)
    keep_ref[0] = jnp.ones((128, 128), F32)
    keep_ref[1] = jnp.where(above, 1.0, 0.0).astype(F32)
    acc_ref[...] = jnp.zeros_like(acc_ref)
    tile_setup(pool_ref, sum_scr, near_scr, far_scr, feat_ref, lhs_ref, rhs_ref, place_ref, wide_ref)

    def add(block, slot, value):
        at = pl.multiple_of(block * (8 * ACC_GROUPS) + 8 * slot, 8)
        acc_ref[pl.ds(at, 8), :] += value

    def step(t, _):
        near, far = pairs_ref[0, 0, 0, t], pairs_ref[0, 0, 1, t]
        keep = jnp.where(near == far, 1, 0)
        w = tile_work(near, far, feat_ref, lhs_ref, rhs_ref, place_ref, wide_ref, keep_ref, keep)
        tile_sums(w, near, far, feat_ref, add)
        return 0

    lax.fori_loop(0, count_ref[0, 0], step, 0)

    def load(slot, row):
        return acc_ref[pl.ds(8 * slot + row, ROWS, stride=8 * ACC_GROUPS), :]

    force, torque = finish_sums(load, pool_features([pool_ref[c] for c in range(13)]))
    for c, rows in enumerate(force + torque):
        own_out[c] = rows[0:8]
        for k in range(3):
            halo_out[k, 4 * c : 4 * c + 4, :] = rows[8 + 4 * k : 12 + 4 * k]


def face_rows_of(face_ref):
    return [face_ref[0, 0, k : k + 1, j * 128 : (j + 1) * 128] for k in range(3) for j in range(4)]


def returned_rows(back_ref, comps):
    return [[back_ref[k, 4 * c + j : 4 * c + j + 1, :] for k in range(3) for j in range(4)] for c in range(comps)]


def frame_body(own_ref, back_ref, pool_x_ref, import_ref, face_ref, frame_ref, force_out, halo_out):
    blocks, lanes = face_masks(face_rows_of(face_ref))
    added = scatter_faces(returned_rows(back_ref, 6), blocks, lanes)
    owned = [own_ref[c] + added[c] for c in range(6)]
    torque = owned[3:6]
    index = [
        jnp.concatenate([frame_ref[0, 0, m : m + 1, b * 128 : (b + 1) * 128] for b in range(OWN_BLOCKS)], axis=0)
        for m in range(3)
    ]
    low = [i & 127 for i in index]
    high = [i >> 7 for i in index]
    spots = [[jnp.zeros((8, 128), F32) for _ in range(3)] for _ in range(3)]
    for b in range(POOL_BLOCKS):
        rows = []
        for c in range(3):
            if b < OWN_BLOCKS:
                rows.append(pool_x_ref[c, b : b + 1, :])
            else:
                k, j = divmod(b - OWN_BLOCKS, 4)
                rows.append(import_ref[k, 4 * c + j : 4 * c + j + 1, :])
        for m in range(3):
            hit = high[m] == b
            for c in range(3):
                spots[m][c] = jnp.where(hit, lane_gather(rows[c], low[m]), spots[m][c])
    place = [pool_x_ref[c] for c in range(3)]
    sub24 = lax.broadcasted_iota(jnp.int32, (ROWS, 128), 0)
    sub128 = lax.broadcasted_iota(jnp.int32, (128, 128), 0)
    kept = [jnp.zeros((8, 128), F32) for _ in range(3)]
    columns, hot = [], []
    for m in range(3):
        lever = [spots[m][c] - place[c] for c in range(3)]
        scale = 1.0 / (3.0 * (dot3(lever, lever) + LEVER_SOFT))
        push = [w * scale for w in cross3(torque, lever)]
        kept = [kept[c] + push[c] for c in range(3)]
        halves = [split2(w) for w in push]
        for b in range(OWN_BLOCKS):
            hit = jnp.broadcast_to(high[m][b : b + 1], (ROWS, 128)) == sub24
            parts = []
            for c in range(3):
                for half in halves[c]:
                    parts.append(jnp.where(hit, jnp.broadcast_to(half[b : b + 1], (ROWS, 128)), 0.0))
            columns.append(jnp.concatenate(parts, axis=0).astype(BF16))
            lane = jnp.broadcast_to(low[m][b : b + 1], (128, 128)) == sub128
            hot.append(jnp.where(lane, 1.0, 0.0).astype(BF16))
    out = nt_dot(jnp.concatenate(columns, axis=1), jnp.concatenate(hot, axis=1))
    for c in range(3):
        rows = out[48 * c : 48 * c + 24] + out[48 * c + 24 : 48 * c + 48]
        force_out[c] = owned[c] + rows[0:8] - kept[c]
        for k in range(3):
            halo_out[k, 4 * c : 4 * c + 4, :] = rows[8 + 4 * k : 12 + 4 * k]
        halo_out[:, 12:16, :] = jnp.zeros((3, 4, 128), F32)


def final_body(force_ref, back_ref, face_ref, out_ref):
    blocks, lanes = face_masks(face_rows_of(face_ref))
    added = scatter_faces(returned_rows(back_ref, 3), blocks, lanes)
    for c in range(3):
        total = force_ref[c] + added[c]
        for b in range(OWN_BLOCKS):
            out_ref[0, 0, c : c + 1, b * 128 : (b + 1) * 128] = total[b : b + 1]


def vmem(count):
    return [pl.BlockSpec(memory_space=pltpu.VMEM)] * count


def shape(*dims):
    return jax.ShapeDtypeStruct(dims, F32)


def exchange(array, step, sizes, collective):
    def body(send_ref, recv_ref, send_sem, recv_sem):
        exchange_body(step, sizes, send_ref, recv_ref, send_sem, recv_sem)

    return pl.pallas_call(
        body,
        out_shape=jax.ShapeDtypeStruct(array.shape, array.dtype),
        in_specs=vmem(1),
        out_specs=pl.BlockSpec(memory_space=pltpu.VMEM),
        scratch_shapes=[pltpu.SemaphoreType.DMA((3,)), pltpu.SemaphoreType.DMA((3,))],
        compiler_params=pltpu.CompilerParams(collective_id=collective, has_side_effects=True),
    )(array)


def gather_exports(coords, multipoles, face_atoms):
    return pl.pallas_call(
        export_body,
        out_shape=(shape(13, 8, 128), shape(3, 56, 128)),
        in_specs=vmem(3),
        out_specs=vmem(2),
    )(coords, multipoles, face_atoms)


def pair_tiles(own, imports, tile_pairs, tile_count):
    return pl.pallas_call(
        tiles_body,
        out_shape=(shape(6, 8, 128), shape(3, 24, 128)),
        in_specs=vmem(2) + [pl.BlockSpec(memory_space=pltpu.SMEM)] * 2,
        out_specs=vmem(2),
        scratch_shapes=[
            pltpu.VMEM((13, ROWS, 128), F32),
            pltpu.VMEM((64 * ROWS, 128), F32),
            pltpu.VMEM((88 * 8, 128), F32),
            pltpu.VMEM((184 * ROWS, 128), F32),
            pltpu.VMEM((POOL_BLOCKS, 128, 128), BF16),
            pltpu.VMEM((OWN_BLOCKS, 128, 384), BF16),
            pltpu.VMEM((POOL_BLOCKS, 128, 896), BF16),
            pltpu.VMEM((POOL_BLOCKS, 8, 128), F32),
            pltpu.VMEM((OWN_BLOCKS, 3, 128, 128), F32),
            pltpu.VMEM((2, 128, 128), F32),
            pltpu.VMEM((ROWS * 8 * ACC_GROUPS, 128), F32),
        ],
        compiler_params=pltpu.CompilerParams(vmem_limit_bytes=48 << 20),
    )(own, imports, tile_pairs, tile_count)


def frame_forces(owned, back, own, imports, face_atoms, frame_atoms):
    return pl.pallas_call(
        frame_body,
        out_shape=(shape(3, 8, 128), shape(3, 16, 128)),
        in_specs=vmem(6),
        out_specs=vmem(2),
    )(owned, back, own, imports, face_atoms, frame_atoms)


def final_forces(force, back, face_atoms):
    return pl.pallas_call(
        final_body,
        out_shape=shape(1, 1, 3, 1024),
        in_specs=vmem(3),
        out_specs=pl.BlockSpec(memory_space=pltpu.VMEM),
    )(force, back, face_atoms)


def solution(mesh):
    sizes = (mesh.shape["gx"], mesh.shape["gy"])

    def shards(coords, multipoles, face_atoms, tile_pairs, tile_count, frame_atoms, send_list, send_count):
        own, exports = gather_exports(coords, multipoles, face_atoms)
        imports = exchange(exports, -1, sizes, 0)
        owned, halo = pair_tiles(own, imports, tile_pairs, tile_count)
        back = exchange(halo, 1, sizes, 1)
        force, spread = frame_forces(owned, back, own, imports, face_atoms, frame_atoms)
        frame_back = exchange(spread, 1, sizes, 2)
        return final_forces(force, frame_back, face_atoms)

    four = P("gx", "gy", None, None)
    placed = (four, four, four, four, P("gx", "gy"), four, four, P("gx", "gy", None))
    return jax.shard_map(shards, mesh=mesh, in_specs=placed, out_specs=four, check_vma=False)
```

time: 431 us -> 76.6 us (0.18)
  the two profiles are of different devices: /device:TPU:6 before, /device:TPU:1 now
where the time goes in v1:
time: 76.6 us; the launch traced here: 75.8 us
  Pallas kernels  67.1 us (88%)
  local copies, waits for them, and re-layouts  7.95 us (10%)
    pallas_call x3, Pallas kernels, exchange(): pl.pallas_call(body, out_shape=jax.ShapeDtypeStruct(array.shape, array.dt...  39.7 us
    pallas_call x1, Pallas kernels, pair_tiles(): pl.pallas_call(tiles_body, out_shape=(shape(6, 8, 128), shape(3, 24, 128)...  21.7 us
    unnamed x16, local copies, waits for them, and re-layouts  6.62 us
    pallas_call x1, Pallas kernels, frame_forces(): pl.pallas_call(frame_body, out_shape=(shape(3, 8, 128), shape(3, 16, 128)...  2.35 us
    pallas_call x1, Pallas kernels, gather_exports(): pl.pallas_call(export_body, out_shape=(shape(13, 8, 128), shape(3, 56, 12...  1.84 us
    pallas_call x1, Pallas kernels, final_forces(): pl.pallas_call(final_body, out_shape=shape(1, 1, 3, 1024), in_specs=vmem(...  1.6 us

profile of v1, /device:TPU:1, one launch (start us, length us, event | category | flops | bytes accessed | tf_op | source)
XLA Modules:
  0.0 75.8 jit_solution(8487163822547794410)
XLA Ops:
  0.0 0.0 copy-start.5
  0.7 1.3 %copy.9.face_ref = s32[1,1,3,512]{3,2,1,0:T(4,128)} copy(s32[1,1,3,512]{3,1,2,0:T(1,128)} %param.10) | data formatting | bytes 12288 | tf_op args[2]
  2.0 1.3 %copy.7.coords_ref = f32[1,1,3,1024]{3,2,1,0:T(4,128)} copy(f32[1,1,3,1024]{3,1,2,0:T(1,128)} %param.8) | data formatting | bytes 24576 | tf_op args[0]
  3.3 1.3 %copy.11.frame_ref = s32[1,1,3,1024]{3,2,1,0:T(4,128)} copy(s32[1,1,3,1024]{3,1,2,0:T(1,128)} %param.13) | data formatting | bytes 24576 | tf_op args[5]
  4.6 0.0 copy-done.5
  4.6 0.6 copy.8.mult_ref
  5.2 1.8 %shard_map.64 = (f32[13,8,128]{2,1,0:T(8,128)}, f32[3,56,128]{2,1,0:T(8,128)}) custom-call(f32[1,1,3,1024]{3,2,1,0:T(4,128)} %copy.7.coords_ref, f32[1,1,10,1024]{3,2,1,0:T(8,128)} %copy.8.mult_ref, s32[1,1,3,512]{3,2,1,0:T(4,128)} %copy.9.face_ref), custom_call_target="tpu_custom_call" | custom-call | tf_op jit(solution)/shard_map/pallas_call | solution.py:576
  7.0 0.0 copy-start.1
  7.0 0.0 copy-start.4
  7.0 11.9 %shard_map.65.import_ref = f32[3,56,128]{2,1,0:T(8,128)} custom-call(f32[3,56,128]{2,1,0:T(8,128)} %get-tuple-element.12.send_ref), custom_call_target="tpu_custom_call" | custom-call | tf_op jit(solution)/shard_map/pallas_call | solution.py:565
  19.0 0.0 copy-done.1
  19.0 0.0 copy-done.4
  19.0 0.0 copy-start
  19.0 0.9 %copy-done = f32[3,56,128]{2,1,0:T(8,128)S(1)} copy-done((f32[3,56,128]{2,1,0:T(8,128)S(1)}, f32[3,56,128]{2,1,0:T(8,128)}, u32[]{:S(2)}) %copy-start) | copy-done | bytes 86040
  19.9 21.7 %shard_map.66 = (f32[6,8,128]{2,1,0:T(8,128)S(1)}, f32[3,24,128]{2,1,0:T(8,128)S(1)}) custom-call(f32[13,8,128]{2,1,0:T(8,128)S(1)} %copy-done.1, f32[3,56,128]{2,1,0:T(8,128)S(1)} %copy-done, s32[1,1,2,32]{3,2,1,0:T(2,128)S(1)} %copy-done.4, s32[1,1]{1,0:T(1,128)S(6)} %copy.14.count_ref), custom_call_target="tpu_custom_call" | custom-call | tf_op jit(solution)/shard_map/pallas_call | solution.py:585
  41.6 0.0 copy-start.2
  41.6 0.6 copy-done.2
  42.2 0.0 copy-start.3
  42.2 0.6 copy-done.3
  42.8 17.7 %shard_map.67.back_ref = f32[3,24,128]{2,1,0:T(8,128)} custom-call(f32[3,24,128]{2,1,0:T(8,128)} %copy-done.2), custom_call_target="tpu_custom_call" | custom-call | tf_op jit(solution)/shard_map/pallas_call | solution.py:565
  60.5 2.4 %shard_map.68 = (f32[3,8,128]{2,1,0:T(8,128)}, f32[3,16,128]{2,1,0:T(8,128)}) custom-call(f32[6,8,128]{2,1,0:T(8,128)} %copy-done.3, f32[3,24,128]{2,1,0:T(8,128)} %shard_map.67.back_ref, f32[13,8,128]{2,1,0:T(8,128)} %get-tuple-element.11.own_ref.pool_x_ref, f32[3,56,128]{2,1,0:T(8,128)} %shard_map.65.import_ref, s32[1,1,3,512]{3,2,1,0:T(4,128)} %copy.9.face_ref, ...), custom_call_target="tpu_custom_call" | custom-call | tf_op jit(solution)/shard_map/pallas_call | solution.py:608
  62.8 10.1 %shard_map.69.back_ref = f32[3,16,128]{2,1,0:T(8,128)} custom-call(f32[3,16,128]{2,1,0:T(8,128)} %get-tuple-element.16.send_ref), custom_call_target="tpu_custom_call" | custom-call | tf_op jit(solution)/shard_map/pallas_call | solution.py:565
  72.9 1.6 %shard_map.70 = f32[1,1,3,1024]{3,2,1,0:T(4,128)} custom-call(f32[3,8,128]{2,1,0:T(8,128)} %get-tuple-element.15.force_ref, f32[3,16,128]{2,1,0:T(8,128)} %shard_map.69.back_ref, s32[1,1,3,512]{3,2,1,0:T(4,128)} %copy.9.face_ref), custom_call_target="tpu_custom_call" | custom-call | tf_op jit(solution)/shard_map/pallas_call | solution.py:617
  74.5 1.3 %copy.13 = f32[1,1,3,1024]{3,1,2,0:T(1,128)} copy(f32[1,1,3,1024]{3,2,1,0:T(4,128)} %shard_map.70) | data formatting | bytes 24576 | tf_op jit(solution)/shard_map/pallas_call | solution.py:617
Async XLA Ops:
  0.0 4.6 %copy-start.5 = (f32[1,1,10,1024]{3,1,2,0:T(1,128)S(1)}, f32[1,1,10,1024]{3,1,2,0:T(1,128)}, u32[]{:S(2)}) copy-start(f32[1,1,10,1024]{3,1,2,0:T(1,128)} %param.9) | copy-start | bytes 122884
  7.0 11.9 %copy-start.1 = (f32[13,8,128]{2,1,0:T(8,128)S(1)}, f32[13,8,128]{2,1,0:T(8,128)}, u32[]{:S(2)}) copy-start(f32[13,8,128]{2,1,0:T(8,128)} %get-tuple-element.11.own_ref.pool_x_ref) | copy-start | bytes 159748
  7.0 11.9 %copy-start.4 = (s32[1,1,2,32]{3,2,1,0:T(2,128)S(1)}, s32[1,1,2,32]{3,2,1,0:T(2,128)}, u32[]{:S(2)}) copy-start(s32[1,1,2,32]{3,2,1,0:T(2,128)} %pairs_ref.1) | copy-start | bytes 772
  19.0 0.9 %copy-start = (f32[3,56,128]{2,1,0:T(8,128)S(1)}, f32[3,56,128]{2,1,0:T(8,128)}, u32[]{:S(2)}) copy-start(f32[3,56,128]{2,1,0:T(8,128)} %shard_map.65.import_ref) | copy-start | bytes 258052
  41.6 0.6 copy-start.2
  42.2 0.6 copy-start.3

commit v2 on v1

--- a/solution.py
+++ b/solution.py
@@ -1,3 +1,5 @@
+import functools
+
 import jax
 import jax.numpy as jnp
 from jax import lax
@@ -94,52 +96,22 @@
     return [out[16 * c : 16 * c + 8] + out[16 * c + 8 : 16 * c + 16] for c in range(comps)]
 
 
-def export_body(coords_ref, mult_ref, face_ref, own_ref, out_ref):
-    for c in range(13):
-        src, row = (coords_ref, c) if c < 3 else (mult_ref, c - 3)
-        for b in range(OWN_BLOCKS):
-            own_ref[c, b : b + 1, :] = src[0, 0, row : row + 1, b * 128 : (b + 1) * 128]
-    face = jnp.concatenate(
-        [face_ref[0, 0, k : k + 1, j * 128 : (j + 1) * 128] for k in range(3) for j in range(4)]
-        + [jnp.zeros((4, 128), jnp.int32)],
-        axis=0,
-    )
-    shift = lax.broadcasted_iota(jnp.int32, (16, 128), 0)
-    shift_x = jnp.where((shift < 4) | (shift >= 8), 1.0, 0.0).astype(F32)
-    shift_y = jnp.where(shift >= 4, 1.0, 0.0).astype(F32)
-    halves = [face[0:8], face[8:16]]
-    lows = [h & 127 for h in halves]
-    highs = [h >> 7 for h in halves]
-    for c in range(13):
-        got = []
-        for part in range(2):
-            total = jnp.zeros((8, 128), F32)
-            for b in range(OWN_BLOCKS):
-                picked = lane_gather(own_ref[c, b : b + 1, :], lows[part])
-                total = jnp.where(highs[part] == b, picked, total)
-            got.append(total)
-        rows = jnp.concatenate(got, axis=0)
-        if c == 0:
-            rows = rows + shift_x
-        if c == 1:
-            rows = rows + shift_y
-        for k in range(3):
-            out_ref[k, 4 * c : 4 * c + 4, :] = rows[4 * k : 4 * k + 4]
-
-
-def exchange_body(step, sizes, send_ref, recv_ref, send_sem, recv_sem):
+def neighbours(sizes):
     gx, gy = lax.axis_index("gx"), lax.axis_index("gy")
     nx, ny = sizes
     up = (lax.rem(gx + 1, nx), lax.rem(gy + 1, ny))
     down = (lax.rem(gx + nx - 1, nx), lax.rem(gy + ny - 1, ny))
-    to = up if step > 0 else down
-    barrier = pltpu.get_barrier_semaphore()
-    for other in (up, down):
-        for peer in ((other[0], gy), (gx, other[1]), (other[0], other[1])):
-            pl.semaphore_signal(barrier, inc=1, device_id=peer, device_id_type=MESH)
-    pl.semaphore_wait(barrier, 6)
+    return [[(to[0], gy), (gx, to[1]), (to[0], to[1])] for to in (up, down)]
+
+
+def greet(senders):
+    for peer in senders:
+        pl.semaphore_signal(pltpu.get_barrier_semaphore(), inc=1, device_id=peer, device_id_type=MESH)
+
+
+def send_sets(send_ref, recv_ref, send_sem, recv_sem, targets):
     copies = []
-    for k, peer in enumerate(((to[0], gy), (gx, to[1]), (to[0], to[1]))):
+    for k, peer in enumerate(targets):
         copy = pltpu.make_async_remote_copy(
             src_ref=send_ref.at[k],
             dst_ref=recv_ref.at[k],
@@ -150,7 +122,39 @@
         )
         copy.start()
         copies.append(copy)
-    for copy in copies:
+    return copies
+
+
+def import_body(sizes, coords_ref, mult_ref, face_ref, recv_ref, send_ref, send_sem, recv_sem):
+    up, down = neighbours(sizes)
+    greet(up)
+    face = jnp.concatenate([face_ref[k] for k in range(3)] + [jnp.zeros((4, 128), jnp.int32)], axis=0)
+    shift = lax.broadcasted_iota(jnp.int32, (16, 128), 0)
+    shift_x = jnp.where((shift < 4) | (shift >= 8), 1.0, 0.0).astype(F32)
+    shift_y = jnp.where(shift >= 4, 1.0, 0.0).astype(F32)
+    halves = [face[0:8], face[8:16]]
+    lows = [h & 127 for h in halves]
+    highs = [h >> 7 for h in halves]
+    for c in range(13):
+        src, at = (coords_ref, 8 * c) if c < 3 else (mult_ref, 8 * (c - 3))
+        got = []
+        for part in range(2):
+            total = jnp.zeros((8, 128), F32)
+            for b in range(OWN_BLOCKS):
+                picked = lane_gather(src[at + b : at + b + 1, :], lows[part])
+                total = jnp.where(highs[part] == b, picked, total)
+            got.append(total)
+        rows = jnp.concatenate(got, axis=0)
+        if c == 0:
+            rows = rows + shift_x
+        if c == 1:
+            rows = rows + shift_y
+        for k in range(3):
+            send_ref[k, 4 * c : 4 * c + 4, :] = rows[4 * k : 4 * k + 4]
+    for k in range(3):
+        send_ref[k, 52:56, :] = jnp.zeros((4, 128), F32)
+    pl.semaphore_wait(pltpu.get_barrier_semaphore(), 3)
+    for copy in send_sets(send_ref, recv_ref, send_sem, recv_sem, down):
         copy.wait()
 
 
@@ -443,11 +447,12 @@
 
 
 def tiles_body(
-    own_ref, import_ref, pairs_ref, count_ref, own_out, halo_out,
+    coords_ref, mult_ref, import_ref, pairs_ref, count_ref, own_out, halo_out,
     pool_ref, sum_scr, near_scr, far_scr, feat_ref, lhs_ref, rhs_ref, place_ref, wide_ref, keep_ref, acc_ref,
 ):
     for c in range(13):
-        pool_ref[c, 0:8, :] = own_ref[c]
+        src, at = (coords_ref, 8 * c) if c < 3 else (mult_ref, 8 * (c - 3))
+        pool_ref[c, 0:8, :] = src[at : at + 8, :]
         for k in range(3):
             pool_ref[c, 8 + 4 * k : 12 + 4 * k, :] = import_ref[k, 4 * c : 4 * c + 4, :]
         pool_ref[c, 20:24, :] = jnp.zeros((4, 128), F32)
@@ -480,23 +485,21 @@
             halo_out[k, 4 * c : 4 * c + 4, :] = rows[8 + 4 * k : 12 + 4 * k]
 
 
-def face_rows_of(face_ref):
-    return [face_ref[0, 0, k : k + 1, j * 128 : (j + 1) * 128] for k in range(3) for j in range(4)]
-
-
 def returned_rows(back_ref, comps):
     return [[back_ref[k, 4 * c + j : 4 * c + j + 1, :] for k in range(3) for j in range(4)] for c in range(comps)]
 
 
-def frame_body(own_ref, back_ref, pool_x_ref, import_ref, face_ref, frame_ref, force_out, halo_out):
-    blocks, lanes = face_masks(face_rows_of(face_ref))
-    added = scatter_faces(returned_rows(back_ref, 6), blocks, lanes)
-    owned = [own_ref[c] + added[c] for c in range(6)]
-    torque = owned[3:6]
-    index = [
-        jnp.concatenate([frame_ref[0, 0, m : m + 1, b * 128 : (b + 1) * 128] for b in range(OWN_BLOCKS)], axis=0)
-        for m in range(3)
-    ]
+def frame_body(
+    sizes, own_ref, halo_ref, coords_ref, import_ref, face_ref, frame_ref, out_ref,
+    back_ref, spread_ref, last_ref, send_sem, recv_sem,
+):
+    up, down = neighbours(sizes)
+    greet(down)
+    pl.semaphore_wait(pltpu.get_barrier_semaphore(), 3)
+    copies = send_sets(halo_ref, back_ref, send_sem.at[0], recv_sem.at[0], up)
+
+    blocks, lanes = face_masks([face_ref[k, j : j + 1, :] for k in range(3) for j in range(4)])
+    index = [frame_ref[8 * m : 8 * m + 8, :] for m in range(3)]
     low = [i & 127 for i in index]
     high = [i >> 7 for i in index]
     spots = [[jnp.zeros((8, 128), F32) for _ in range(3)] for _ in range(3)]
@@ -504,7 +507,7 @@
         rows = []
         for c in range(3):
             if b < OWN_BLOCKS:
-                rows.append(pool_x_ref[c, b : b + 1, :])
+                rows.append(coords_ref[8 * c + b : 8 * c + b + 1, :])
             else:
                 k, j = divmod(b - OWN_BLOCKS, 4)
                 rows.append(import_ref[k, 4 * c + j : 4 * c + j + 1, :])
@@ -512,42 +515,52 @@
             hit = high[m] == b
             for c in range(3):
                 spots[m][c] = jnp.where(hit, lane_gather(rows[c], low[m]), spots[m][c])
-    place = [pool_x_ref[c] for c in range(3)]
+    place = [coords_ref[8 * c : 8 * c + 8, :] for c in range(3)]
+    levers, scales = [], []
+    for m in range(3):
+        lever = [spots[m][c] - place[c] for c in range(3)]
+        levers.append(lever)
+        scales.append(1.0 / (3.0 * (dot3(lever, lever) + LEVER_SOFT)))
     sub24 = lax.broadcasted_iota(jnp.int32, (ROWS, 128), 0)
     sub128 = lax.broadcasted_iota(jnp.int32, (128, 128), 0)
+    hits, hot = [], []
+    for m in range(3):
+        for b in range(OWN_BLOCKS):
+            hits.append(jnp.broadcast_to(high[m][b : b + 1], (ROWS, 128)) == sub24)
+            lane = jnp.broadcast_to(low[m][b : b + 1], (128, 128)) == sub128
+            hot.append(jnp.where(lane, 1.0, 0.0).astype(BF16))
+
+    for copy in copies:
+        copy.wait()
+    added = scatter_faces(returned_rows(back_ref, 6), blocks, lanes)
+    owned = [own_ref[c] + added[c] for c in range(6)]
+    torque = owned[3:6]
     kept = [jnp.zeros((8, 128), F32) for _ in range(3)]
-    columns, hot = [], []
+    columns = []
     for m in range(3):
-        lever = [spots[m][c] - place[c] for c in range(3)]
-        scale = 1.0 / (3.0 * (dot3(lever, lever) + LEVER_SOFT))
-        push = [w * scale for w in cross3(torque, lever)]
+        push = [w * scales[m] for w in cross3(torque, levers[m])]
         kept = [kept[c] + push[c] for c in range(3)]
         halves = [split2(w) for w in push]
         for b in range(OWN_BLOCKS):
-            hit = jnp.broadcast_to(high[m][b : b + 1], (ROWS, 128)) == sub24
+            hit = hits[8 * m + b]
             parts = []
             for c in range(3):
                 for half in halves[c]:
                     parts.append(jnp.where(hit, jnp.broadcast_to(half[b : b + 1], (ROWS, 128)), 0.0))
             columns.append(jnp.concatenate(parts, axis=0).astype(BF16))
-            lane = jnp.broadcast_to(low[m][b : b + 1], (128, 128)) == sub128
-            hot.append(jnp.where(lane, 1.0, 0.0).astype(BF16))
     out = nt_dot(jnp.concatenate(columns, axis=1), jnp.concatenate(hot, axis=1))
+    forces = []
     for c in range(3):
         rows = out[48 * c : 48 * c + 24] + out[48 * c + 24 : 48 * c + 48]
-        force_out[c] = owned[c] + rows[0:8] - kept[c]
+        forces.append(owned[c] + rows[0:8] - kept[c])
         for k in range(3):
-            halo_out[k, 4 * c : 4 * c + 4, :] = rows[8 + 4 * k : 12 + 4 * k]
-        halo_out[:, 12:16, :] = jnp.zeros((3, 4, 128), F32)
-
-
-def final_body(force_ref, back_ref, face_ref, out_ref):
-    blocks, lanes = face_masks(face_rows_of(face_ref))
-    added = scatter_faces(returned_rows(back_ref, 3), blocks, lanes)
+            spread_ref[k, 4 * c : 4 * c + 4, :] = rows[8 + 4 * k : 12 + 4 * k]
+    spread_ref[:, 12:16, :] = jnp.zeros((3, 4, 128), F32)
+    for copy in send_sets(spread_ref, last_ref, send_sem.at[1], recv_sem.at[1], up):
+        copy.wait()
+    added = scatter_faces(returned_rows(last_ref, 3), blocks, lanes)
     for c in range(3):
-        total = force_ref[c] + added[c]
-        for b in range(OWN_BLOCKS):
-            out_ref[0, 0, c : c + 1, b * 128 : (b + 1) * 128] = total[b : b + 1]
+        out_ref[8 * c : 8 * c + 8, :] = forces[c] + added[c]
 
 
 def vmem(count):
@@ -558,34 +571,26 @@
     return jax.ShapeDtypeStruct(dims, F32)
 
 
-def exchange(array, step, sizes, collective):
-    def body(send_ref, recv_ref, send_sem, recv_sem):
-        exchange_body(step, sizes, send_ref, recv_ref, send_sem, recv_sem)
-
+def import_halo(sizes, coords, multipoles, face_atoms):
     return pl.pallas_call(
-        body,
-        out_shape=jax.ShapeDtypeStruct(array.shape, array.dtype),
-        in_specs=vmem(1),
+        functools.partial(import_body, sizes),
+        out_shape=shape(3, 56, 128),
+        in_specs=vmem(3),
         out_specs=pl.BlockSpec(memory_space=pltpu.VMEM),
-        scratch_shapes=[pltpu.SemaphoreType.DMA((3,)), pltpu.SemaphoreType.DMA((3,))],
-        compiler_params=pltpu.CompilerParams(collective_id=collective, has_side_effects=True),
-    )(array)
-
-
-def gather_exports(coords, multipoles, face_atoms):
-    return pl.pallas_call(
-        export_body,
-        out_shape=(shape(13, 8, 128), shape(3, 56, 128)),
-        in_specs=vmem(3),
-        out_specs=vmem(2),
+        scratch_shapes=[
+            pltpu.VMEM((3, 56, 128), F32),
+            pltpu.SemaphoreType.DMA((3,)),
+            pltpu.SemaphoreType.DMA((3,)),
+        ],
+        compiler_params=pltpu.CompilerParams(collective_id=0, has_side_effects=True),
     )(coords, multipoles, face_atoms)
 
 
-def pair_tiles(own, imports, tile_pairs, tile_count):
+def pair_tiles(coords, multipoles, imports, tile_pairs, tile_count):
     return pl.pallas_call(
         tiles_body,
         out_shape=(shape(6, 8, 128), shape(3, 24, 128)),
-        in_specs=vmem(2) + [pl.BlockSpec(memory_space=pltpu.SMEM)] * 2,
+        in_specs=vmem(3) + [pl.BlockSpec(memory_space=pltpu.SMEM)] * 2,
         out_specs=vmem(2),
         scratch_shapes=[
             pltpu.VMEM((13, ROWS, 128), F32),
@@ -601,38 +606,38 @@
             pltpu.VMEM((ROWS * 8 * ACC_GROUPS, 128), F32),
         ],
         compiler_params=pltpu.CompilerParams(vmem_limit_bytes=48 << 20),
-    )(own, imports, tile_pairs, tile_count)
-
-
-def frame_forces(owned, back, own, imports, face_atoms, frame_atoms):
+    )(coords, multipoles, imports, tile_pairs, tile_count)
+
+
+def frame_forces(sizes, owned, halo, coords, imports, face_atoms, frame_atoms):
     return pl.pallas_call(
-        frame_body,
-        out_shape=(shape(3, 8, 128), shape(3, 16, 128)),
+        functools.partial(frame_body, sizes),
+        out_shape=shape(24, 128),
         in_specs=vmem(6),
-        out_specs=vmem(2),
-    )(owned, back, own, imports, face_atoms, frame_atoms)
-
-
-def final_forces(force, back, face_atoms):
-    return pl.pallas_call(
-        final_body,
-        out_shape=shape(1, 1, 3, 1024),
-        in_specs=vmem(3),
         out_specs=pl.BlockSpec(memory_space=pltpu.VMEM),
-    )(force, back, face_atoms)
+        scratch_shapes=[
+            pltpu.VMEM((3, 24, 128), F32),
+            pltpu.VMEM((3, 16, 128), F32),
+            pltpu.VMEM((3, 16, 128), F32),
+            pltpu.SemaphoreType.DMA((2, 3)),
+            pltpu.SemaphoreType.DMA((2, 3)),
+        ],
+        compiler_params=pltpu.CompilerParams(collective_id=1, has_side_effects=True),
+    )(owned, halo, coords, imports, face_atoms, frame_atoms)
 
 
 def solution(mesh):
     sizes = (mesh.shape["gx"], mesh.shape["gy"])
 
     def shards(coords, multipoles, face_atoms, tile_pairs, tile_count, frame_atoms, send_list, send_count):
-        own, exports = gather_exports(coords, multipoles, face_atoms)
-        imports = exchange(exports, -1, sizes, 0)
-        owned, halo = pair_tiles(own, imports, tile_pairs, tile_count)
-        back = exchange(halo, 1, sizes, 1)
-        force, spread = frame_forces(owned, back, own, imports, face_atoms, frame_atoms)
-        frame_back = exchange(spread, 1, sizes, 2)
-        return final_forces(force, frame_back, face_atoms)
+        coords = coords.reshape(24, 128)
+        multipoles = multipoles.reshape(80, 128)
+        face_atoms = face_atoms.reshape(3, 4, 128)
+        frame_atoms = frame_atoms.reshape(24, 128)
+        imports = import_halo(sizes, coords, multipoles, face_atoms)
+        owned, halo = pair_tiles(coords, multipoles, imports, tile_pairs, tile_count)
+        forces = frame_forces(sizes, owned, halo, coords, imports, face_atoms, frame_atoms)
+        return forces.reshape(1, 1, 3, 1024)
 
     four = P("gx", "gy", None, None)
     placed = (four, four, four, four, P("gx", "gy"), four, four, P("gx", "gy", None))

time: 76.6 us -> 60.1 us (0.78)
  Pallas kernels: 67.1 us -> 55.6 us
  local copies, waits for them, and re-layouts: 7.95 us -> 3.41 us
    pallas_call x6 -> x2, Pallas kernels: 45.4 us -> 39.1 us  [the longest x1 27.3 us: frame_forces(): pl.pallas_call(functools.partial(frame_body, sizes), out_shape=shape(24,...]
    pallas_call x1, Pallas kernels: 21.7 us -> 16.5 us  [pair_tiles(): pl.pallas_call(tiles_body, out_shape=(shape(6, 8, 128), shape(3, 24, 128)...]
    unnamed x16 -> x13, local copies, waits for them, and re-layouts: 6.62 us -> 3.41 us
    pallas_call x1 -> x0, local copies, waits for them, and re-layouts: 1.33 us -> none  [final_forces(): pl.pallas_call(final_body, out_shape=shape(1, 1, 3, 1024), in_specs=vmem(...]
where the time goes in v2:
time: 60.1 us; the launch traced here: 59.7 us
  Pallas kernels  55.6 us (93%)
  local copies, waits for them, and re-layouts  3.41 us (6%)
  between operations  0.74 us (1%)
    pallas_call x1, Pallas kernels, frame_forces(): pl.pallas_call(functools.partial(frame_body, sizes), out_shape=shape(24,...  27.3 us
    pallas_call x1, Pallas kernels, pair_tiles(): pl.pallas_call(tiles_body, out_shape=(shape(6, 8, 128), shape(3, 24, 128)...  16.5 us
    pallas_call x1, Pallas kernels, import_halo(): pl.pallas_call(functools.partial(import_body, sizes), out_shape=shape(3,...  11.8 us
    unnamed x13, local copies, waits for them, and re-layouts  3.41 us

profile of v2, /device:TPU:1, one launch (start us, length us, event | category | flops | bytes accessed | tf_op | source)
XLA Modules:
  0.0 59.7 jit_solution(866614342561357178)
XLA Ops:
  0.7 0.0 copy-start.1
  0.7 0.0 copy-start.2
  0.7 0.0 copy-start.5
  0.7 11.8 %shard_map.64.import_ref = f32[3,56,128]{2,1,0:T(8,128)} custom-call(f32[24,128]{1,0:T(8,128)} %bitcast.7, f32[80,128]{1,0:T(8,128)} %bitcast.5, s32[3,4,128]{2,1,0:T(4,128)} %bitcast.11), custom_call_target="tpu_custom_call" | custom-call | tf_op jit(solution)/shard_map/pallas_call | solution.py:575
  12.5 0.0 copy-done.1
  12.5 0.0 copy-done.2
  12.5 0.0 copy-done.5
  12.5 0.0 copy-start
  12.5 0.9 %copy-done = f32[3,56,128]{2,1,0:T(8,128)S(1)} copy-done((f32[3,56,128]{2,1,0:T(8,128)S(1)}, f32[3,56,128]{2,1,0:T(8,128)}, u32[]{:S(2)}) %copy-start) | copy-done | bytes 86040
  13.4 16.5 %shard_map.65 = (f32[6,8,128]{2,1,0:T(8,128)S(1)}, f32[3,24,128]{2,1,0:T(8,128)S(1)}) custom-call(f32[24,128]{1,0:T(8,128)S(1)} %bitcast.9, f32[80,128]{1,0:T(8,128)S(1)} %bitcast.6, f32[3,56,128]{2,1,0:T(8,128)S(1)} %copy-done, s32[1,1,2,32]{3,2,1,0:T(2,128)S(1)} %copy-done.5, s32[1,1]{1,0:T(1,128)S(6)} %copy.10.count_ref), custom_call_target="tpu_custom_call" | custom-call | tf_op jit(solution)/shard_map/pallas_call | solution.py:590
  29.9 0.0 copy-start.3
  30.0 0.6 %copy-done.3 = f32[3,24,128]{2,1,0:T(8,128)} copy-done((f32[3,24,128]{2,1,0:T(8,128)}, f32[3,24,128]{2,1,0:T(8,128)S(1)}, u32[]{:S(2)}) %copy-start.3) | copy-done | bytes 36888
  30.6 0.0 copy-start.4
  30.6 0.6 copy-done.4
  31.2 27.3 %shard_map.66 = f32[24,128]{1,0:T(8,128)} custom-call(f32[6,8,128]{2,1,0:T(8,128)} %copy-done.4, f32[3,24,128]{2,1,0:T(8,128)} %copy-done.3, f32[24,128]{1,0:T(8,128)} %bitcast.8, f32[3,56,128]{2,1,0:T(8,128)} %shard_map.64.import_ref, s32[3,4,128]{2,1,0:T(4,128)} %bitcast.12, s32[24,128]{1,0:T(8,128)} %bitcast.13), custom_call_target="tpu_custom_call" | custom-call | tf_op jit(solution)/shard_map/pallas_call | solution.py:613
  58.4 1.3 %copy.11 = f32[1,1,3,1024]{3,1,2,0:T(1,128)} copy(f32[1,1,3,1024]{3,1,2,0:T(1,128)} %bitcast.10) | data formatting | bytes 24576
Async XLA Ops:
  0.7 11.8 %copy-start.1 = (f32[1,1,10,1024]{3,1,2,0:T(1,128)S(1)}, f32[1,1,10,1024]{3,1,2,0:T(1,128)}, u32[]{:S(2)}) copy-start(f32[1,1,10,1024]{3,1,2,0:T(1,128)} %param.9) | copy-start | bytes 122884
  0.7 11.8 %copy-start.2 = (f32[1,1,3,1024]{3,1,2,0:T(1,128)S(1)}, f32[1,1,3,1024]{3,1,2,0:T(1,128)}, u32[]{:S(2)}) copy-start(f32[1,1,3,1024]{3,1,2,0:T(1,128)} %param.8) | copy-start | bytes 36868
  0.7 11.8 %copy-start.5 = (s32[1,1,2,32]{3,2,1,0:T(2,128)S(1)}, s32[1,1,2,32]{3,2,1,0:T(2,128)}, u32[]{:S(2)}) copy-start(s32[1,1,2,32]{3,2,1,0:T(2,128)} %pairs_ref.1) | copy-start | bytes 772
  12.5 0.9 %copy-start = (f32[3,56,128]{2,1,0:T(8,128)S(1)}, f32[3,56,128]{2,1,0:T(8,128)}, u32[]{:S(2)}) copy-start(f32[3,56,128]{2,1,0:T(8,128)} %shard_map.64.import_ref) | copy-start | bytes 258052
  29.9 0.6 %copy-start.3 = (f32[3,24,128]{2,1,0:T(8,128)}, f32[3,24,128]{2,1,0:T(8,128)S(1)}, u32[]{:S(2)}) copy-start(f32[3,24,128]{2,1,0:T(8,128)S(1)} %get-tuple-element.8.halo_ref) | copy-start | bytes 110596
  30.6 0.6 %copy-start.4 = (f32[6,8,128]{2,1,0:T(8,128)}, f32[6,8,128]{2,1,0:T(8,128)S(1)}, u32[]{:S(2)}) copy-start(f32[6,8,128]{2,1,0:T(8,128)S(1)} %get-tuple-element.7.own_ref) | copy-start | bytes 73732

commit v3 on v2

--- a/solution.py
+++ b/solution.py
@@ -222,14 +222,14 @@
         + [9.0 * q]
         + [9.0 * MULT[e] * quad[e] for e in range(6)]
     )
-    l3 = [-180.0 * MULT[e] * f["tx"][e] for e in range(6)] + [180.0 * turned[r] for r in range(3)]
-    l3 += [-180.0 * MULT[e] * quad[e] for e in range(6)]
+    l3 = [-252.0 * MULT[e] * f["tx"][e] for e in range(6)] + [252.0 * turned[r] for r in range(3)]
+    l3 += [-252.0 * MULT[e] * quad[e] for e in range(6)]
     for a, b in ENTRIES:
         for c in range(3):
             term = quad[ENTRY_AT[(a, c)]] * x[b]
             if a != b:
                 term = term + quad[ENTRY_AT[(b, c)]] * x[a]
-            l3.append(180.0 * term)
+            l3.append(252.0 * term)
     l3 += z(7)
     return [u, v, p, r_, l1, l2, l3]
 
@@ -264,7 +264,7 @@
             rhs_ref[b, :, out_id * 128 : (out_id + 1) * 128] = stacked
         return 0
 
-    lax.fori_loop(0, POOL_BLOCKS, per_block, 0)
+    lax.fori_loop(0, POOL_BLOCKS, per_block, 0, unroll=4)
 
     def per_near(b, _):
         start = 0
@@ -279,7 +279,7 @@
             wide_ref[b, r] = jnp.broadcast_to(place[:, r + 1 : r + 2], (128, 128))
         return 0
 
-    lax.fori_loop(0, OWN_BLOCKS, per_near, 0)
+    lax.fori_loop(0, OWN_BLOCKS, per_near, 0, unroll=4)
 
 
 def tile_work(near, far, feat_ref, lhs_ref, rhs_ref, place_ref, wide_ref, keep_ref, keep):
@@ -300,16 +300,15 @@
         b1 = b0 * t
         b2 = b1 * t
         b3 = b2 * t
-        b4 = b3 * (1.4 * t)
-        b5 = b4 * (1.8 * t)
         u, v = first[rows, 0:128], first[rows, 128:256]
-        p, r_ = first[rows, 256:384], first[rows, 384:512]
+        pt, rt = first[rows, 256:384] * t, first[rows, 384:512] * t
         l1, l2, l3 = second[rows, 0:128], second[rows, 128:256], third[rows, :]
-        al = r_ * b3 - v * b2
-        be = p * b3 + u * b2
-        ga = r_ * b4 - v * b3
-        de = p * b4 + u * b3
-        e1 = l1 * b2 + (l2 - u * v) * b3 + (u * r_ - v * p + l3) * b4 + (p * r_) * b5
+        gr, gp = 1.4 * rt - v, 1.4 * pt + u
+        al = b2 * (rt - v)
+        be = b2 * (pt + u)
+        ga = b3 * gr
+        de = b3 * gp
+        e1 = b2 * (l1 + t * (l2 + gr * gp + 0.56 * (rt * pt) + t * l3))
         for name, value in zip(names, (b1, b2, b3, al, be, ga, de, e1)):
             hi = value.astype(BF16)
             pieces[name][0].append(hi)
@@ -336,9 +335,9 @@
             lhs = jnp.concatenate([feats, feats], axis=1)
             if transposed:
                 rhs = jnp.concatenate(
-                    [jnp.concatenate(w[one], axis=1), jnp.concatenate(w[two], axis=1)], axis=0
+                    [jnp.concatenate([w[one][s].T, w[two][s].T], axis=1) for s in range(2)], axis=0
                 )
-                out = nt_dot(lhs, rhs)
+                out = mm(lhs, rhs)
             else:
                 rhs = jnp.concatenate(
                     [jnp.concatenate([w[one][s], w[two][s]], axis=1) for s in range(2)], axis=0
@@ -459,6 +458,7 @@
     above = lax.broadcasted_iota(jnp.int32, (128, 128), 0) < lax.broadcasted_iota(jnp.int32, (128, 128), 1)
     keep_ref[0] = jnp.ones((128, 128), F32)
     keep_ref[1] = jnp.where(above, 1.0, 0.0).astype(F32)
+    keep_ref[2] = jnp.zeros((128, 128), F32)
     acc_ref[...] = jnp.zeros_like(acc_ref)
     tile_setup(pool_ref, sum_scr, near_scr, far_scr, feat_ref, lhs_ref, rhs_ref, place_ref, wide_ref)
 
@@ -466,14 +466,23 @@
         at = pl.multiple_of(block * (8 * ACC_GROUPS) + 8 * slot, 8)
         acc_ref[pl.ds(at, 8), :] += value
 
-    def step(t, _):
+    def one(t):
         near, far = pairs_ref[0, 0, 0, t], pairs_ref[0, 0, 1, t]
-        keep = jnp.where(near == far, 1, 0)
+        keep = jnp.where(t < count_ref[0, 0], jnp.where(near == far, 1, 0), 2)
         w = tile_work(near, far, feat_ref, lhs_ref, rhs_ref, place_ref, wide_ref, keep_ref, keep)
-        tile_sums(w, near, far, feat_ref, add)
+        return near, far, w
+
+    def step(g, _):
+        prev = None
+        for n in range(8):
+            cur = one(8 * g + n)
+            if prev is not None:
+                tile_sums(prev[2], prev[0], prev[1], feat_ref, add)
+            prev = cur
+        tile_sums(prev[2], prev[0], prev[1], feat_ref, add)
         return 0
 
-    lax.fori_loop(0, count_ref[0, 0], step, 0)
+    lax.fori_loop(0, (count_ref[0, 0] + 7) // 8, step, 0)
 
     def load(slot, row):
         return acc_ref[pl.ds(8 * slot + row, ROWS, stride=8 * ACC_GROUPS), :]
@@ -602,7 +611,7 @@
             pltpu.VMEM((POOL_BLOCKS, 128, 896), BF16),
             pltpu.VMEM((POOL_BLOCKS, 8, 128), F32),
             pltpu.VMEM((OWN_BLOCKS, 3, 128, 128), F32),
-            pltpu.VMEM((2, 128, 128), F32),
+            pltpu.VMEM((3, 128, 128), F32),
             pltpu.VMEM((ROWS * 8 * ACC_GROUPS, 128), F32),
         ],
         compiler_params=pltpu.CompilerParams(vmem_limit_bytes=48 << 20),

time: 60.1 us -> 52.3 us (0.87)
  Pallas kernels: 55.6 us -> 47.8 us
    pallas_call x1, Pallas kernels: 27.3 us -> 23.1 us  [frame_forces(): pl.pallas_call(functools.partial(frame_body, sizes), out_shape=shape(24,...]
    pallas_call x1, Pallas kernels: 16.5 us -> 12.9 us  [pair_tiles(): pl.pallas_call(tiles_body, out_shape=(shape(6, 8, 128), shape(3, 24, 128)...]
where the time goes in v3:
time: 52.3 us; the launch traced here: 51.9 us
  Pallas kernels  47.8 us (91%)
  local copies, waits for them, and re-layouts  3.41 us (7%)
  between operations  0.74 us (1%)
    pallas_call x1, Pallas kernels, frame_forces(): pl.pallas_call(functools.partial(frame_body, sizes), out_shape=shape(24,...  23.1 us
    pallas_call x1, Pallas kernels, pair_tiles(): pl.pallas_call(tiles_body, out_shape=(shape(6, 8, 128), shape(3, 24, 128)...  12.9 us
    pallas_call x1, Pallas kernels, import_halo(): pl.pallas_call(functools.partial(import_body, sizes), out_shape=shape(3,...  11.8 us
    unnamed x13, local copies, waits for them, and re-layouts  3.41 us

profile of v3, /device:TPU:1, one launch (start us, length us, event | category | flops | bytes accessed | tf_op | source)
XLA Modules:
  0.0 51.9 jit_solution(16756169049605991467)
XLA Ops:
  0.7 0.0 copy-start.1
  0.7 0.0 copy-start.2
  0.7 0.0 copy-start.5
  0.7 11.8 %shard_map.64.import_ref = f32[3,56,128]{2,1,0:T(8,128)} custom-call(f32[24,128]{1,0:T(8,128)} %bitcast.7, f32[80,128]{1,0:T(8,128)} %bitcast.5, s32[3,4,128]{2,1,0:T(4,128)} %bitcast.11), custom_call_target="tpu_custom_call" | custom-call | tf_op jit(solution)/shard_map/pallas_call | solution.py:584
  12.5 0.0 copy-done.1
  12.5 0.0 copy-done.2
  12.5 0.0 copy-done.5
  12.5 0.0 copy-start
  12.5 0.9 %copy-done = f32[3,56,128]{2,1,0:T(8,128)S(1)} copy-done((f32[3,56,128]{2,1,0:T(8,128)S(1)}, f32[3,56,128]{2,1,0:T(8,128)}, u32[]{:S(2)}) %copy-start) | copy-done | bytes 86040
  13.4 12.9 %shard_map.65 = (f32[6,8,128]{2,1,0:T(8,128)S(1)}, f32[3,24,128]{2,1,0:T(8,128)S(1)}) custom-call(f32[24,128]{1,0:T(8,128)S(1)} %bitcast.9, f32[80,128]{1,0:T(8,128)S(1)} %bitcast.6, f32[3,56,128]{2,1,0:T(8,128)S(1)} %copy-done, s32[1,1,2,32]{3,2,1,0:T(2,128)S(1)} %copy-done.5, s32[1,1]{1,0:T(1,128)S(6)} %copy.10.count_ref), custom_call_target="tpu_custom_call" | custom-call | tf_op jit(solution)/shard_map/pallas_call | solution.py:599
  26.3 0.0 copy-start.3
  26.3 0.6 %copy-done.3 = f32[3,24,128]{2,1,0:T(8,128)} copy-done((f32[3,24,128]{2,1,0:T(8,128)}, f32[3,24,128]{2,1,0:T(8,128)S(1)}, u32[]{:S(2)}) %copy-start.3) | copy-done | bytes 36888
  26.9 0.0 copy-start.4
  26.9 0.6 %copy-done.4 = f32[6,8,128]{2,1,0:T(8,128)} copy-done((f32[6,8,128]{2,1,0:T(8,128)}, f32[6,8,128]{2,1,0:T(8,128)S(1)}, u32[]{:S(2)}) %copy-start.4) | copy-done | bytes 24600
  27.5 23.1 %shard_map.66 = f32[24,128]{1,0:T(8,128)} custom-call(f32[6,8,128]{2,1,0:T(8,128)} %copy-done.4, f32[3,24,128]{2,1,0:T(8,128)} %copy-done.3, f32[24,128]{1,0:T(8,128)} %bitcast.8, f32[3,56,128]{2,1,0:T(8,128)} %shard_map.64.import_ref, s32[3,4,128]{2,1,0:T(4,128)} %bitcast.12, s32[24,128]{1,0:T(8,128)} %bitcast.13), custom_call_target="tpu_custom_call" | custom-call | tf_op jit(solution)/shard_map/pallas_call | solution.py:622
  50.6 1.3 %copy.11 = f32[1,1,3,1024]{3,1,2,0:T(1,128)} copy(f32[1,1,3,1024]{3,1,2,0:T(1,128)} %bitcast.10) | data formatting | bytes 24576
Async XLA Ops:
  0.7 11.8 %copy-start.1 = (f32[1,1,10,1024]{3,1,2,0:T(1,128)S(1)}, f32[1,1,10,1024]{3,1,2,0:T(1,128)}, u32[]{:S(2)}) copy-start(f32[1,1,10,1024]{3,1,2,0:T(1,128)} %param.9) | copy-start | bytes 122884
  0.7 11.8 %copy-start.2 = (f32[1,1,3,1024]{3,1,2,0:T(1,128)S(1)}, f32[1,1,3,1024]{3,1,2,0:T(1,128)}, u32[]{:S(2)}) copy-start(f32[1,1,3,1024]{3,1,2,0:T(1,128)} %param.8) | copy-start | bytes 36868
  0.7 11.8 %copy-start.5 = (s32[1,1,2,32]{3,2,1,0:T(2,128)S(1)}, s32[1,1,2,32]{3,2,1,0:T(2,128)}, u32[]{:S(2)}) copy-start(s32[1,1,2,32]{3,2,1,0:T(2,128)} %pairs_ref.1) | copy-start | bytes 772
  12.5 0.9 %copy-start = (f32[3,56,128]{2,1,0:T(8,128)S(1)}, f32[3,56,128]{2,1,0:T(8,128)}, u32[]{:S(2)}) copy-start(f32[3,56,128]{2,1,0:T(8,128)} %shard_map.64.import_ref) | copy-start | bytes 258052
  26.3 0.6 %copy-start.3 = (f32[3,24,128]{2,1,0:T(8,128)}, f32[3,24,128]{2,1,0:T(8,128)S(1)}, u32[]{:S(2)}) copy-start(f32[3,24,128]{2,1,0:T(8,128)S(1)} %get-tuple-element.8.halo_ref) | copy-start | bytes 110596
  26.9 0.6 %copy-start.4 = (f32[6,8,128]{2,1,0:T(8,128)}, f32[6,8,128]{2,1,0:T(8,128)S(1)}, u32[]{:S(2)}) copy-start(f32[6,8,128]{2,1,0:T(8,128)S(1)} %get-tuple-element.7.own_ref) | copy-start | bytes 73732

commit v4 on v3

--- a/solution.py
+++ b/solution.py
@@ -18,6 +18,8 @@
 F32 = jnp.float32
 BF16 = jnp.bfloat16
 ACC_GROUPS = 18
+EVENTS = 64
+TILE_STEP = 8
 MESH = pl.DeviceIdType.MESH
 
 
@@ -123,39 +125,6 @@
         copy.start()
         copies.append(copy)
     return copies
-
-
-def import_body(sizes, coords_ref, mult_ref, face_ref, recv_ref, send_ref, send_sem, recv_sem):
-    up, down = neighbours(sizes)
-    greet(up)
-    face = jnp.concatenate([face_ref[k] for k in range(3)] + [jnp.zeros((4, 128), jnp.int32)], axis=0)
-    shift = lax.broadcasted_iota(jnp.int32, (16, 128), 0)
-    shift_x = jnp.where((shift < 4) | (shift >= 8), 1.0, 0.0).astype(F32)
-    shift_y = jnp.where(shift >= 4, 1.0, 0.0).astype(F32)
-    halves = [face[0:8], face[8:16]]
-    lows = [h & 127 for h in halves]
-    highs = [h >> 7 for h in halves]
-    for c in range(13):
-        src, at = (coords_ref, 8 * c) if c < 3 else (mult_ref, 8 * (c - 3))
-        got = []
-        for part in range(2):
-            total = jnp.zeros((8, 128), F32)
-            for b in range(OWN_BLOCKS):
-                picked = lane_gather(src[at + b : at + b + 1, :], lows[part])
-                total = jnp.where(highs[part] == b, picked, total)
-            got.append(total)
-        rows = jnp.concatenate(got, axis=0)
-        if c == 0:
-            rows = rows + shift_x
-        if c == 1:
-            rows = rows + shift_y
-        for k in range(3):
-            send_ref[k, 4 * c : 4 * c + 4, :] = rows[4 * k : 4 * k + 4]
-    for k in range(3):
-        send_ref[k, 52:56, :] = jnp.zeros((4, 128), F32)
-    pl.semaphore_wait(pltpu.get_barrier_semaphore(), 3)
-    for copy in send_sets(send_ref, recv_ref, send_sem, recv_sem, down):
-        copy.wait()
 
 
 def pool_features(pool):
@@ -234,52 +203,47 @@
     return [u, v, p, r_, l1, l2, l3]
 
 
-def tile_setup(pool_ref, sum_scr, near_scr, far_scr, feat_ref, lhs_ref, rhs_ref, place_ref, wide_ref):
-    f = pool_features([pool_ref[c] for c in range(13)])
+def far_block(b, sum_scr, far_scr, feat_ref, rhs_ref, place_ref):
+    sums = sum_scr[pl.ds(b, 64, stride=ROWS), :]
+    place_ref[b] = sums[0:8]
+    hi, lo = split2(sums)
+    parts = []
+    for g in range(8):
+        parts += [hi[8 * g : 8 * g + 8], lo[8 * g : 8 * g + 8]]
+    feat_ref[b] = jnp.concatenate(parts, axis=0).astype(BF16)
+    start = 0
+    for out_id, count in enumerate((24, 24, 24, 24, 24, 24, 40)):
+        rows = far_scr[pl.ds(b + start * ROWS, count, stride=ROWS), :]
+        start += count
+        hi, lo = split2(rows)
+        pad = [jnp.zeros((128 - 3 * count, 128), F32)]
+        stacked = jnp.concatenate([hi, lo, hi] + pad, axis=0).astype(BF16)
+        rhs_ref[b, :, out_id * 128 : (out_id + 1) * 128] = stacked
+
+
+def near_block(b, near_scr, lhs_ref, place_ref, wide_ref):
+    start = 0
+    for group, count in enumerate((24, 24, 40)):
+        rows = near_scr[pl.ds(b + start * 8, count, stride=8), :]
+        start += count
+        hi, lo = split2(rows)
+        stacked = jnp.concatenate([hi, hi, lo, jnp.zeros((128 - 3 * count, 128), F32)], axis=0)
+        lhs_ref[b, :, group * 128 : (group + 1) * 128] = stacked.T.astype(BF16)
+    place = jnp.concatenate([place_ref[b], jnp.zeros((120, 128), F32)], axis=0).T
+    for r in range(3):
+        wide_ref[b, r] = jnp.broadcast_to(place[:, r + 1 : r + 2], (128, 128))
+
+
+def store_rows(pool, low, high, sum_scr, far_scr):
+    f = pool_features([pool[c][low:high] for c in range(13)])
     for n, row in enumerate(sum_rows(f)):
-        sum_scr[n * ROWS : (n + 1) * ROWS, :] = row
-    for n, row in enumerate(near_rows(f)):
-        near_scr[n * 8 : n * 8 + 8, :] = row[0:8]
+        sum_scr[n * ROWS + low : n * ROWS + high, :] = row
     at = 0
     for group in far_rows(f):
         for row in group:
-            far_scr[at * ROWS : (at + 1) * ROWS, :] = row
+            far_scr[at * ROWS + low : at * ROWS + high, :] = row
             at += 1
-
-    def per_block(b, _):
-        sums = sum_scr[pl.ds(b, 64, stride=ROWS), :]
-        place_ref[b] = sums[0:8]
-        hi, lo = split2(sums)
-        parts = []
-        for g in range(8):
-            parts += [hi[8 * g : 8 * g + 8], lo[8 * g : 8 * g + 8]]
-        feat_ref[b] = jnp.concatenate(parts, axis=0).astype(BF16)
-        start = 0
-        for out_id, count in enumerate((24, 24, 24, 24, 24, 24, 40)):
-            rows = far_scr[pl.ds(b + start * ROWS, count, stride=ROWS), :]
-            start += count
-            hi, lo = split2(rows)
-            pad = [jnp.zeros((128 - 3 * count, 128), F32)]
-            stacked = jnp.concatenate([hi, lo, hi] + pad, axis=0).astype(BF16)
-            rhs_ref[b, :, out_id * 128 : (out_id + 1) * 128] = stacked
-        return 0
-
-    lax.fori_loop(0, POOL_BLOCKS, per_block, 0, unroll=4)
-
-    def per_near(b, _):
-        start = 0
-        for group, count in enumerate((24, 24, 40)):
-            rows = near_scr[pl.ds(b + start * 8, count, stride=8), :]
-            start += count
-            hi, lo = split2(rows)
-            stacked = jnp.concatenate([hi, hi, lo, jnp.zeros((128 - 3 * count, 128), F32)], axis=0)
-            lhs_ref[b, :, group * 128 : (group + 1) * 128] = stacked.T.astype(BF16)
-        place = jnp.concatenate([place_ref[b], jnp.zeros((120, 128), F32)], axis=0).T
-        for r in range(3):
-            wide_ref[b, r] = jnp.broadcast_to(place[:, r + 1 : r + 2], (128, 128))
-        return 0
-
-    lax.fori_loop(0, OWN_BLOCKS, per_near, 0, unroll=4)
+    return f
 
 
 def tile_work(near, far, feat_ref, lhs_ref, rhs_ref, place_ref, wide_ref, keep_ref, keep):
@@ -329,7 +293,7 @@
         ("b2", "ga", 64, ((5, 0), (6, 1), (7, 2), (8, 3)), ((9, 2), (10, 3))),
         ("de", "b3", 128, ((11, 0), (12, 7)), ((13, 2), (14, 3), (15, 4), (16, 5), (17, 6))),
     )
-    for pairs, source, target, transposed in ((near_pairs, far, near, True), (far_pairs, near, far, False)):
+    for pairs, source, side, transposed in ((near_pairs, far, 0, True), (far_pairs, near, 1, False)):
         for one, two, rows, slots_one, slots_two in pairs:
             feats = feat_ref[source, 0:rows, :]
             lhs = jnp.concatenate([feats, feats], axis=1)
@@ -347,7 +311,7 @@
                 lanes = slice(128 * half, 128 * half + 128)
                 for slot, group in slots:
                     at = 16 * group
-                    add(target, slot, out[at : at + 8, lanes] + out[at + 8 : at + 16, lanes])
+                    add(side, slot, out[at : at + 8, lanes] + out[at + 8 : at + 16, lanes])
 
 
 def finish_sums(load, f):
@@ -445,67 +409,160 @@
     return force, torque
 
 
-def tiles_body(
-    coords_ref, mult_ref, import_ref, pairs_ref, count_ref, own_out, halo_out,
-    pool_ref, sum_scr, near_scr, far_scr, feat_ref, lhs_ref, rhs_ref, place_ref, wide_ref, keep_ref, acc_ref,
-):
+def gather_exports(coords_ref, mult_ref, face_ref, send_ref):
+    face = jnp.concatenate([face_ref[k] for k in range(3)] + [jnp.zeros((4, 128), jnp.int32)], axis=0)
+    shift = lax.broadcasted_iota(jnp.int32, (16, 128), 0)
+    shift_x = jnp.where((shift < 4) | (shift >= 8), 1.0, 0.0).astype(F32)
+    shift_y = jnp.where(shift >= 4, 1.0, 0.0).astype(F32)
+    halves = [face[0:8], face[8:16]]
+    lows = [h & 127 for h in halves]
+    highs = [h >> 7 for h in halves]
     for c in range(13):
         src, at = (coords_ref, 8 * c) if c < 3 else (mult_ref, 8 * (c - 3))
-        pool_ref[c, 0:8, :] = src[at : at + 8, :]
+        got = []
+        for part in range(2):
+            total = jnp.zeros((8, 128), F32)
+            for b in range(OWN_BLOCKS):
+                picked = lane_gather(src[at + b : at + b + 1, :], lows[part])
+                total = jnp.where(highs[part] == b, picked, total)
+            got.append(total)
+        rows = jnp.concatenate(got, axis=0)
+        if c == 0:
+            rows = rows + shift_x
+        if c == 1:
+            rows = rows + shift_y
         for k in range(3):
-            pool_ref[c, 8 + 4 * k : 12 + 4 * k, :] = import_ref[k, 4 * c : 4 * c + 4, :]
+            send_ref[k, 4 * c : 4 * c + 4, :] = rows[4 * k : 4 * k + 4]
+    for k in range(3):
+        send_ref[k, 52:56, :] = jnp.zeros((4, 128), F32)
+
+
+def event_tables(pairs_ref, table_ref):
+    lane = lax.broadcasted_iota(jnp.int32, (8, 128), 1)
+    blocks = [pairs_ref[0, 0, e % 2, e // 2] for e in range(EVENTS)]
+    row = jnp.zeros((8, 128), jnp.int32)
+    for e, block in enumerate(blocks):
+        row = jnp.where(lane == e, block, row)
+    before = jnp.full((8, 128), EVENTS, jnp.int32)
+    last = jnp.full((8, 128), EVENTS, jnp.int32)
+    for e, block in enumerate(blocks):
+        before = jnp.where((row == block) & (lane > e), e, before)
+        last = jnp.where(lane == block, e, last)
+    sub = lax.broadcasted_iota(jnp.int32, (8, 128), 0)
+    table_ref[...] = jnp.where(sub == 0, before, last)
+
+
+def returned_rows(back_ref, comps):
+    return [[back_ref[k, 4 * c + j : 4 * c + j + 1, :] for k in range(3) for j in range(4)] for c in range(comps)]
+
+
+def kernel_body(
+    sizes, coords_hbm, mult_hbm, face_hbm, frame_hbm, pairs_hbm, count_hbm, out_ref,
+    coords_ref, mult_ref, face_ref, frame_ref, pairs_ref, count_ref, load_sem, send_ref, import_ref, halo_ref, back_ref, spread_ref, last_ref, table_ref, smem_ref,
+    pool_ref, sum_scr, near_scr, far_scr, feat_ref, lhs_ref, rhs_ref, place_ref, wide_ref, keep_ref, runs_ref, acc_ref,
+    send_sem, recv_sem, back_send, back_recv, last_send, last_recv, local_sem,
+):
+    up, down = neighbours(sizes)
+    greet(up)
+    loads = [
+        pltpu.make_async_copy(source, target, load_sem.at[n])
+        for n, (source, target) in enumerate(
+            (
+                (coords_hbm, coords_ref),
+                (mult_hbm, mult_ref),
+                (face_hbm, face_ref),
+                (frame_hbm, frame_ref),
+                (pairs_hbm, pairs_ref),
+                (count_hbm, count_ref),
+            )
+        )
+    ]
+    for copy in loads:
+        copy.start()
+    for copy in loads:
+        copy.wait()
+    gather_exports(coords_ref, mult_ref, face_ref, send_ref)
+    pl.semaphore_wait(pltpu.get_barrier_semaphore(), 3)
+    copies = send_sets(send_ref, import_ref, send_sem, recv_sem, down)
+
+    event_tables(pairs_ref, table_ref)
+    table_copy = pltpu.make_async_copy(table_ref, smem_ref, local_sem)
+    table_copy.start()
+    own = [coords_ref[8 * c : 8 * c + 8, :] for c in range(3)] + [mult_ref[8 * c : 8 * c + 8, :] for c in range(10)]
+    for c in range(13):
+        pool_ref[c, 0:8, :] = own[c]
         pool_ref[c, 20:24, :] = jnp.zeros((4, 128), F32)
+    f = store_rows(own, 0, 8, sum_scr, far_scr)
+    for n, row in enumerate(near_rows(f)):
+        near_scr[n * 8 : n * 8 + 8, :] = row
     above = lax.broadcasted_iota(jnp.int32, (128, 128), 0) < lax.broadcasted_iota(jnp.int32, (128, 128), 1)
     keep_ref[0] = jnp.ones((128, 128), F32)
     keep_ref[1] = jnp.where(above, 1.0, 0.0).astype(F32)
     keep_ref[2] = jnp.zeros((128, 128), F32)
-    acc_ref[...] = jnp.zeros_like(acc_ref)
-    tile_setup(pool_ref, sum_scr, near_scr, far_scr, feat_ref, lhs_ref, rhs_ref, place_ref, wide_ref)
-
-    def add(block, slot, value):
-        at = pl.multiple_of(block * (8 * ACC_GROUPS) + 8 * slot, 8)
-        acc_ref[pl.ds(at, 8), :] += value
+    runs_ref[EVENTS] = jnp.zeros((ACC_GROUPS, 8, 128), F32)
+    for b in range(POOL_BLOCKS, ROWS):
+        acc_ref[b * 8 * ACC_GROUPS : (b + 1) * 8 * ACC_GROUPS, :] = jnp.zeros((8 * ACC_GROUPS, 128), F32)
+
+    def own_block(b, _):
+        far_block(b, sum_scr, far_scr, feat_ref, rhs_ref, place_ref)
+        near_block(b, near_scr, lhs_ref, place_ref, wide_ref)
+        return 0
+
+    lax.fori_loop(0, OWN_BLOCKS, own_block, 0, unroll=4)
+    table_copy.wait()
+
+    for copy in copies:
+        copy.wait()
+    for c in range(13):
+        for k in range(3):
+            pool_ref[c, 8 + 4 * k : 12 + 4 * k, :] = import_ref[k, 4 * c : 4 * c + 4, :]
+    store_rows([pool_ref[c] for c in range(13)], 8, 24, sum_scr, far_scr)
+
+    def import_block(b, _):
+        far_block(b + OWN_BLOCKS, sum_scr, far_scr, feat_ref, rhs_ref, place_ref)
+        return 0
+
+    lax.fori_loop(0, POOL_BLOCKS - OWN_BLOCKS, import_block, 0, unroll=4)
 
     def one(t):
         near, far = pairs_ref[0, 0, 0, t], pairs_ref[0, 0, 1, t]
         keep = jnp.where(t < count_ref[0, 0], jnp.where(near == far, 1, 0), 2)
-        w = tile_work(near, far, feat_ref, lhs_ref, rhs_ref, place_ref, wide_ref, keep_ref, keep)
-        return near, far, w
+        return t, near, far, tile_work(near, far, feat_ref, lhs_ref, rhs_ref, place_ref, wide_ref, keep_ref, keep)
+
+    def sums(t, near, far, w):
+        before = [smem_ref[0, 2 * t + side] for side in range(2)]
+
+        def add(side, slot, value):
+            runs_ref[2 * t + side, slot] = runs_ref[before[side], slot] + value
+
+        tile_sums(w, near, far, feat_ref, add)
 
     def step(g, _):
-        prev = None
-        for n in range(8):
-            cur = one(8 * g + n)
-            if prev is not None:
-                tile_sums(prev[2], prev[0], prev[1], feat_ref, add)
-            prev = cur
-        tile_sums(prev[2], prev[0], prev[1], feat_ref, add)
+        held = None
+        for n in range(TILE_STEP):
+            current = one(TILE_STEP * g + n)
+            if held is not None:
+                sums(*held)
+            held = current
+        sums(*held)
         return 0
 
-    lax.fori_loop(0, (count_ref[0, 0] + 7) // 8, step, 0)
+    lax.fori_loop(0, EVENTS // 2 // TILE_STEP, step, 0)
+
+    for b in range(POOL_BLOCKS):
+        at = smem_ref[1, b]
+        for slot in range(ACC_GROUPS):
+            row = (b * ACC_GROUPS + slot) * 8
+            acc_ref[row : row + 8, :] = runs_ref[at, slot]
 
     def load(slot, row):
         return acc_ref[pl.ds(8 * slot + row, ROWS, stride=8 * ACC_GROUPS), :]
 
     force, torque = finish_sums(load, pool_features([pool_ref[c] for c in range(13)]))
     for c, rows in enumerate(force + torque):
-        own_out[c] = rows[0:8]
         for k in range(3):
-            halo_out[k, 4 * c : 4 * c + 4, :] = rows[8 + 4 * k : 12 + 4 * k]
-
-
-def returned_rows(back_ref, comps):
-    return [[back_ref[k, 4 * c + j : 4 * c + j + 1, :] for k in range(3) for j in range(4)] for c in range(comps)]
-
-
-def frame_body(
-    sizes, own_ref, halo_ref, coords_ref, import_ref, face_ref, frame_ref, out_ref,
-    back_ref, spread_ref, last_ref, send_sem, recv_sem,
-):
-    up, down = neighbours(sizes)
-    greet(down)
-    pl.semaphore_wait(pltpu.get_barrier_semaphore(), 3)
-    copies = send_sets(halo_ref, back_ref, send_sem.at[0], recv_sem.at[0], up)
+            halo_ref[k, 4 * c : 4 * c + 4, :] = rows[8 + 4 * k : 12 + 4 * k]
+    copies = send_sets(halo_ref, back_ref, back_send, back_recv, up)
 
     blocks, lanes = face_masks([face_ref[k, j : j + 1, :] for k in range(3) for j in range(4)])
     index = [frame_ref[8 * m : 8 * m + 8, :] for m in range(3)]
@@ -513,21 +570,13 @@
     high = [i >> 7 for i in index]
     spots = [[jnp.zeros((8, 128), F32) for _ in range(3)] for _ in range(3)]
     for b in range(POOL_BLOCKS):
-        rows = []
         for c in range(3):
-            if b < OWN_BLOCKS:
-                rows.append(coords_ref[8 * c + b : 8 * c + b + 1, :])
-            else:
-                k, j = divmod(b - OWN_BLOCKS, 4)
-                rows.append(import_ref[k, 4 * c + j : 4 * c + j + 1, :])
-        for m in range(3):
-            hit = high[m] == b
-            for c in range(3):
-                spots[m][c] = jnp.where(hit, lane_gather(rows[c], low[m]), spots[m][c])
-    place = [coords_ref[8 * c : 8 * c + 8, :] for c in range(3)]
+            row = pool_ref[c, b : b + 1, :]
+            for m in range(3):
+                spots[m][c] = jnp.where(high[m] == b, lane_gather(row, low[m]), spots[m][c])
     levers, scales = [], []
     for m in range(3):
-        lever = [spots[m][c] - place[c] for c in range(3)]
+        lever = [spots[m][c] - own[c] for c in range(3)]
         levers.append(lever)
         scales.append(1.0 / (3.0 * (dot3(lever, lever) + LEVER_SOFT)))
     sub24 = lax.broadcasted_iota(jnp.int32, (ROWS, 128), 0)
@@ -542,7 +591,7 @@
     for copy in copies:
         copy.wait()
     added = scatter_faces(returned_rows(back_ref, 6), blocks, lanes)
-    owned = [own_ref[c] + added[c] for c in range(6)]
+    owned = [rows[0:8] + more for rows, more in zip(force + torque, added)]
     torque = owned[3:6]
     kept = [jnp.zeros((8, 128), F32) for _ in range(3)]
     columns = []
@@ -565,43 +614,37 @@
         for k in range(3):
             spread_ref[k, 4 * c : 4 * c + 4, :] = rows[8 + 4 * k : 12 + 4 * k]
     spread_ref[:, 12:16, :] = jnp.zeros((3, 4, 128), F32)
-    for copy in send_sets(spread_ref, last_ref, send_sem.at[1], recv_sem.at[1], up):
+    for copy in send_sets(spread_ref, last_ref, last_send, last_recv, up):
         copy.wait()
     added = scatter_faces(returned_rows(last_ref, 3), blocks, lanes)
     for c in range(3):
         out_ref[8 * c : 8 * c + 8, :] = forces[c] + added[c]
 
 
-def vmem(count):
-    return [pl.BlockSpec(memory_space=pltpu.VMEM)] * count
-
-
-def shape(*dims):
-    return jax.ShapeDtypeStruct(dims, F32)
-
-
-def import_halo(sizes, coords, multipoles, face_atoms):
+def domain_forces(sizes, coords, multipoles, face_atoms, frame_atoms, tile_pairs, tile_count):
+    vmem = pl.BlockSpec(memory_space=pltpu.VMEM)
+    hbm = pl.BlockSpec(memory_space=pltpu.HBM)
     return pl.pallas_call(
-        functools.partial(import_body, sizes),
-        out_shape=shape(3, 56, 128),
-        in_specs=vmem(3),
-        out_specs=pl.BlockSpec(memory_space=pltpu.VMEM),
+        functools.partial(kernel_body, sizes),
+        out_shape=jax.ShapeDtypeStruct((24, 128), F32),
+        in_specs=[hbm] * 6,
+        out_specs=vmem,
         scratch_shapes=[
+            pltpu.VMEM((24, 128), F32),
+            pltpu.VMEM((80, 128), F32),
+            pltpu.VMEM((3, 4, 128), jnp.int32),
+            pltpu.VMEM((24, 128), jnp.int32),
+            pltpu.SMEM((1, 1, 2, 32), jnp.int32),
+            pltpu.SMEM((1, 1), jnp.int32),
+            pltpu.SemaphoreType.DMA((6,)),
             pltpu.VMEM((3, 56, 128), F32),
-            pltpu.SemaphoreType.DMA((3,)),
-            pltpu.SemaphoreType.DMA((3,)),
-        ],
-        compiler_params=pltpu.CompilerParams(collective_id=0, has_side_effects=True),
-    )(coords, multipoles, face_atoms)
-
-
-def pair_tiles(coords, multipoles, imports, tile_pairs, tile_count):
-    return pl.pallas_call(
-        tiles_body,
-        out_shape=(shape(6, 8, 128), shape(3, 24, 128)),
-        in_specs=vmem(3) + [pl.BlockSpec(memory_space=pltpu.SMEM)] * 2,
-        out_specs=vmem(2),
-        scratch_shapes=[
+            pltpu.VMEM((3, 56, 128), F32),
+            pltpu.VMEM((3, 24, 128), F32),
+            pltpu.VMEM((3, 24, 128), F32),
+            pltpu.VMEM((3, 16, 128), F32),
+            pltpu.VMEM((3, 16, 128), F32),
+            pltpu.VMEM((8, 128), jnp.int32),
+            pltpu.SMEM((8, 128), jnp.int32),
             pltpu.VMEM((13, ROWS, 128), F32),
             pltpu.VMEM((64 * ROWS, 128), F32),
             pltpu.VMEM((88 * 8, 128), F32),
@@ -612,27 +655,13 @@
             pltpu.VMEM((POOL_BLOCKS, 8, 128), F32),
             pltpu.VMEM((OWN_BLOCKS, 3, 128, 128), F32),
             pltpu.VMEM((3, 128, 128), F32),
+            pltpu.VMEM((EVENTS + 1, ACC_GROUPS, 8, 128), F32),
             pltpu.VMEM((ROWS * 8 * ACC_GROUPS, 128), F32),
-        ],
-        compiler_params=pltpu.CompilerParams(vmem_limit_bytes=48 << 20),
-    )(coords, multipoles, imports, tile_pairs, tile_count)
-
-
-def frame_forces(sizes, owned, halo, coords, imports, face_atoms, frame_atoms):
-    return pl.pallas_call(
-        functools.partial(frame_body, sizes),
-        out_shape=shape(24, 128),
-        in_specs=vmem(6),
-        out_specs=pl.BlockSpec(memory_space=pltpu.VMEM),
-        scratch_shapes=[
-            pltpu.VMEM((3, 24, 128), F32),
-            pltpu.VMEM((3, 16, 128), F32),
-            pltpu.VMEM((3, 16, 128), F32),
-            pltpu.SemaphoreType.DMA((2, 3)),
-            pltpu.SemaphoreType.DMA((2, 3)),
-        ],
-        compiler_params=pltpu.CompilerParams(collective_id=1, has_side_effects=True),
-    )(owned, halo, coords, imports, face_atoms, frame_atoms)
+        ]
+        + [pltpu.SemaphoreType.DMA((3,))] * 6
+        + [pltpu.SemaphoreType.DMA],
+        compiler_params=pltpu.CompilerParams(collective_id=0, has_side_effects=True, vmem_limit_bytes=52 << 20),
+    )(coords, multipoles, face_atoms, frame_atoms, tile_pairs, tile_count)
 
 
 def solution(mesh):
@@ -643,9 +672,7 @@
         multipoles = multipoles.reshape(80, 128)
         face_atoms = face_atoms.reshape(3, 4, 128)
         frame_atoms = frame_atoms.reshape(24, 128)
-        imports = import_halo(sizes, coords, multipoles, face_atoms)
-        owned, halo = pair_tiles(coords, multipoles, imports, tile_pairs, tile_count)
-        forces = frame_forces(sizes, owned, halo, coords, imports, face_atoms, frame_atoms)
+        forces = domain_forces(sizes, coords, multipoles, face_atoms, frame_atoms, tile_pairs, tile_count)
         return forces.reshape(1, 1, 3, 1024)
 
     four = P("gx", "gy", None, None)

time: 52.3 us -> 45.4 us (0.87)
  Pallas kernels: 47.8 us -> 40.9 us
    pallas_call x3 -> x1, Pallas kernels: 47.8 us -> 40.9 us  [domain_forces(): pl.pallas_call(functools.partial(kernel_body, sizes), out_shape=jax.Shape...]
    unnamed x13 -> x11, local copies, waits for them, and re-layouts: 3.41 us -> 3.47 us
where the time goes in v4:
time: 45.4 us; the launch traced here: 45.1 us
  Pallas kernels  40.9 us (90%)
  local copies, waits for them, and re-layouts  3.47 us (8%)
  between operations  0.69 us (2%)
    pallas_call x1, Pallas kernels, domain_forces(): pl.pallas_call(functools.partial(kernel_body, sizes), out_shape=jax.Shape...  40.9 us
    unnamed x11, local copies, waits for them, and re-layouts  3.47 us

profile of v4, /device:TPU:1, one launch (start us, length us, event | category | flops | bytes accessed | tf_op | source)
XLA Modules:
  0.0 45.1 jit_solution(7194859412485645045)
XLA Ops:
  0.0 0.0 copy-start.3
  0.7 0.0 copy-start.4
  0.7 0.0 copy-done.3
  0.7 0.7 %copy-done.4 = s32[1,1,2,32]{3,2,1,0:T(2,128)S(1)} copy-done((s32[1,1,2,32]{3,2,1,0:T(2,128)S(1)}, s32[1,1,2,32]{3,2,1,0:T(2,128)}, u32[]{:S(2)}) %copy-start.4) | copy-done | bytes 280
  1.3 0.0 copy-start
  1.4 0.8 %copy-done = f32[1,1,10,1024]{3,1,2,0:T(1,128)S(1)} copy-done((f32[1,1,10,1024]{3,1,2,0:T(1,128)S(1)}, f32[1,1,10,1024]{3,1,2,0:T(1,128)}, u32[]{:S(2)}) %copy-start) | copy-done | bytes 40984
  2.1 0.0 copy-start.1
  2.1 0.7 %copy-done.1 = f32[1,1,3,1024]{3,1,2,0:T(1,128)S(1)} copy-done((f32[1,1,3,1024]{3,1,2,0:T(1,128)S(1)}, f32[1,1,3,1024]{3,1,2,0:T(1,128)}, u32[]{:S(2)}) %copy-start.1) | copy-done | bytes 12312
  2.8 0.0 copy-start.2
  2.8 0.7 %copy-done.2 = s32[1,1,3,1024]{3,1,2,0:T(1,128)S(1)} copy-done((s32[1,1,3,1024]{3,1,2,0:T(1,128)S(1)}, s32[1,1,3,1024]{3,1,2,0:T(1,128)}, u32[]{:S(2)}) %copy-start.2) | copy-done | bytes 12312
  3.5 40.9 %shard_map.64 = f32[24,128]{1,0:T(8,128)S(1)} custom-call(f32[24,128]{1,0:T(8,128)S(1)} %bitcast.7, f32[80,128]{1,0:T(8,128)S(1)} %bitcast.6, s32[3,4,128]{2,1,0:T(4,128)S(1)} %bitcast.9, s32[24,128]{1,0:T(8,128)S(1)} %bitcast.8, s32[1,1,2,32]{3,2,1,0:T(2,128)S(1)} %copy-done.4, s32[1,1]{1,0:T(1,128)S(6)} %copy.10.count_hbm), custom_call_target="tpu_custom_call" | custom-call | tf_op jit(solution)/shard_map/pallas_call | solution.py:627
  44.5 0.6 %copy.11 = f32[1,1,3,1024]{3,1,2,0:T(1,128)} copy(f32[1,1,3,1024]{3,1,2,0:T(1,128)S(1)} %bitcast.5) | data formatting | bytes 24576
Async XLA Ops:
  0.0 0.7 %copy-start.3 = (s32[1,1,3,512]{3,1,2,0:T(1,128)S(1)}, s32[1,1,3,512]{3,1,2,0:T(1,128)}, u32[]{:S(2)}) copy-start(s32[1,1,3,512]{3,1,2,0:T(1,128)} %param.10) | copy-start | bytes 18436
  0.7 0.7 %copy-start.4 = (s32[1,1,2,32]{3,2,1,0:T(2,128)S(1)}, s32[1,1,2,32]{3,2,1,0:T(2,128)}, u32[]{:S(2)}) copy-start(s32[1,1,2,32]{3,2,1,0:T(2,128)} %pairs_hbm.1) | copy-start | bytes 772
  1.3 0.8 %copy-start = (f32[1,1,10,1024]{3,1,2,0:T(1,128)S(1)}, f32[1,1,10,1024]{3,1,2,0:T(1,128)}, u32[]{:S(2)}) copy-start(f32[1,1,10,1024]{3,1,2,0:T(1,128)} %param.9) | copy-start | bytes 122884
  2.1 0.7 %copy-start.1 = (f32[1,1,3,1024]{3,1,2,0:T(1,128)S(1)}, f32[1,1,3,1024]{3,1,2,0:T(1,128)}, u32[]{:S(2)}) copy-start(f32[1,1,3,1024]{3,1,2,0:T(1,128)} %param.8) | copy-start | bytes 36868
  2.8 0.7 %copy-start.2 = (s32[1,1,3,1024]{3,1,2,0:T(1,128)S(1)}, s32[1,1,3,1024]{3,1,2,0:T(1,128)}, u32[]{:S(2)}) copy-start(s32[1,1,3,1024]{3,1,2,0:T(1,128)} %param.13) | copy-start | bytes 36868

commit v5 on v4

--- a/solution.py
+++ b/solution.py
@@ -19,7 +19,7 @@
 BF16 = jnp.bfloat16
 ACC_GROUPS = 18
 EVENTS = 64
-TILE_STEP = 8
+TILE_STEP = 16
 MESH = pl.DeviceIdType.MESH
 
 
@@ -148,11 +148,11 @@
 
 def sum_rows(f):
     zero = jnp.zeros_like(f["one"])
-    rows = [f["one"], *f["x"], f["q"], *f["d"]]
+    rows = [*f["xx"], zero, zero]
+    rows += [f["one"], *f["x"], f["q"], *f["d"]]
     rows += [*f["qx"], *f["m"], zero, zero]
     rows += [*f["quad"], *f["turned"], *f["h"], zero]
     rows += [*f["tx"]] + [f["outer"][e][c] for e in range(6) for c in range(3)]
-    rows += [*f["xx"], zero, zero]
     return rows
 
 
@@ -205,7 +205,7 @@
 
 def far_block(b, sum_scr, far_scr, feat_ref, rhs_ref, place_ref):
     sums = sum_scr[pl.ds(b, 64, stride=ROWS), :]
-    place_ref[b] = sums[0:8]
+    place_ref[b] = sums[8:16]
     hi, lo = split2(sums)
     parts = []
     for g in range(8):
@@ -281,21 +281,30 @@
 
 
 def tile_sums(w, near, far, feat_ref, add):
-    near_pairs = (
-        ("al", "be", 16, ((0, 0),), ((1, 0),)),
-        ("e1", "b1", 32, ((2, 0),), ((3, 0), (4, 1))),
-        ("b2", "de", 64, ((5, 0), (6, 1), (7, 2), (8, 3)), ((9, 2), (10, 3))),
-        ("ga", "b3", 128, ((11, 0), (12, 7)), ((13, 2), (14, 3), (15, 4), (16, 5), (17, 6))),
-    )
-    far_pairs = (
-        ("be", "al", 16, ((0, 0),), ((1, 0),)),
-        ("e1", "b1", 32, ((2, 0),), ((3, 0), (4, 1))),
-        ("b2", "ga", 64, ((5, 0), (6, 1), (7, 2), (8, 3)), ((9, 2), (10, 3))),
-        ("de", "b3", 128, ((11, 0), (12, 7)), ((13, 2), (14, 3), (15, 4), (16, 5), (17, 6))),
-    )
+    slots = {
+        "a": ((0, 1),),
+        "ap": ((1, 1),),
+        "e": ((2, 1),),
+        "b1": ((3, 1), (4, 2)),
+        "b2": ((5, 1), (6, 2), (7, 3), (8, 4)),
+        "cp": ((9, 3), (10, 4)),
+        "c": ((11, 1), (12, 0)),
+        "b3": ((13, 3), (14, 4), (15, 5), (16, 6), (17, 7)),
+    }
+
+    def pairs_for(a, ap, c, cp):
+        return (
+            (a, ap, 1, 2, slots["a"], slots["ap"]),
+            ("e1", c, 0, 2, slots["e"], slots["c"]),
+            ("b1", "b2", 1, 5, slots["b1"], slots["b2"]),
+            (cp, "b3", 3, 8, slots["cp"], slots["b3"]),
+        )
+
+    near_pairs = pairs_for("al", "be", "ga", "de")
+    far_pairs = pairs_for("be", "al", "de", "ga")
     for pairs, source, side, transposed in ((near_pairs, far, 0, True), (far_pairs, near, 1, False)):
-        for one, two, rows, slots_one, slots_two in pairs:
-            feats = feat_ref[source, 0:rows, :]
+        for one, two, first, final, slots_one, slots_two in pairs:
+            feats = feat_ref[source, 16 * first : 16 * final, :]
             lhs = jnp.concatenate([feats, feats], axis=1)
             if transposed:
                 rhs = jnp.concatenate(
@@ -307,10 +316,10 @@
                     [jnp.concatenate([w[one][s], w[two][s]], axis=1) for s in range(2)], axis=0
                 )
                 out = mm(lhs, rhs)
-            for half, slots in enumerate((slots_one, slots_two)):
+            for half, targets in enumerate((slots_one, slots_two)):
                 lanes = slice(128 * half, 128 * half + 128)
-                for slot, group in slots:
-                    at = 16 * group
+                for slot, group in targets:
+                    at = 16 * (group - first)
                     add(side, slot, out[at : at + 8, lanes] + out[at + 8 : at + 16, lanes])
 
 
@@ -452,8 +461,10 @@
     table_ref[...] = jnp.where(sub == 0, before, last)
 
 
-def returned_rows(back_ref, comps):
-    return [[back_ref[k, 4 * c + j : 4 * c + j + 1, :] for k in range(3) for j in range(4)] for c in range(comps)]
+def scatter_sets(back_ref, comps, sets, blocks, lanes):
+    chosen = [(k, j) for k in sets for j in range(4)]
+    values = [[back_ref[k, 4 * c + j : 4 * c + j + 1, :] for k, j in chosen] for c in range(comps)]
+    return scatter_faces(values, [blocks[4 * k + j] for k, j in chosen], [lanes[4 * k + j] for k, j in chosen])
 
 
 def kernel_body(
@@ -511,18 +522,18 @@
     lax.fori_loop(0, OWN_BLOCKS, own_block, 0, unroll=4)
     table_copy.wait()
 
-    for copy in copies:
-        copy.wait()
-    for c in range(13):
-        for k in range(3):
-            pool_ref[c, 8 + 4 * k : 12 + 4 * k, :] = import_ref[k, 4 * c : 4 * c + 4, :]
-    store_rows([pool_ref[c] for c in range(13)], 8, 24, sum_scr, far_scr)
-
     def import_block(b, _):
-        far_block(b + OWN_BLOCKS, sum_scr, far_scr, feat_ref, rhs_ref, place_ref)
+        far_block(b, sum_scr, far_scr, feat_ref, rhs_ref, place_ref)
         return 0
 
-    lax.fori_loop(0, POOL_BLOCKS - OWN_BLOCKS, import_block, 0, unroll=4)
+    for sets, rows, blocks in (((0, 1), (8, 16), (8, 16)), ((2,), (16, 24), (16, 20))):
+        for k in sets:
+            copies[k].wait()
+        for c in range(13):
+            for k in sets:
+                pool_ref[c, 8 + 4 * k : 12 + 4 * k, :] = import_ref[k, 4 * c : 4 * c + 4, :]
+        store_rows([pool_ref[c] for c in range(13)], *rows, sum_scr, far_scr)
+        lax.fori_loop(*blocks, import_block, 0, unroll=4)
 
     def one(t):
         near, far = pairs_ref[0, 0, 0, t], pairs_ref[0, 0, 1, t]
@@ -549,20 +560,25 @@
 
     lax.fori_loop(0, EVENTS // 2 // TILE_STEP, step, 0)
 
-    for b in range(POOL_BLOCKS):
-        at = smem_ref[1, b]
-        for slot in range(ACC_GROUPS):
-            row = (b * ACC_GROUPS + slot) * 8
-            acc_ref[row : row + 8, :] = runs_ref[at, slot]
-
-    def load(slot, row):
-        return acc_ref[pl.ds(8 * slot + row, ROWS, stride=8 * ACC_GROUPS), :]
-
-    force, torque = finish_sums(load, pool_features([pool_ref[c] for c in range(13)]))
-    for c, rows in enumerate(force + torque):
+    def finish(low, high):
+        for b in range(low, min(high, POOL_BLOCKS)):
+            at = smem_ref[1, b]
+            for slot in range(ACC_GROUPS):
+                row = (b * ACC_GROUPS + slot) * 8
+                acc_ref[row : row + 8, :] = runs_ref[at, slot]
+
+        def load(slot, row):
+            at = low * 8 * ACC_GROUPS + 8 * slot + row
+            return acc_ref[pl.ds(at, high - low, stride=8 * ACC_GROUPS), :]
+
+        force, torque = finish_sums(load, pool_features([pool_ref[c, low:high, :] for c in range(13)]))
+        return force + torque
+
+    for c, rows in enumerate(finish(8, 24)):
         for k in range(3):
-            halo_ref[k, 4 * c : 4 * c + 4, :] = rows[8 + 4 * k : 12 + 4 * k]
+            halo_ref[k, 4 * c : 4 * c + 4, :] = rows[4 * k : 4 * k + 4]
     copies = send_sets(halo_ref, back_ref, back_send, back_recv, up)
+    partial = finish(0, 8)
 
     blocks, lanes = face_masks([face_ref[k, j : j + 1, :] for k in range(3) for j in range(4)])
     index = [frame_ref[8 * m : 8 * m + 8, :] for m in range(3)]
@@ -588,10 +604,12 @@
             lane = jnp.broadcast_to(low[m][b : b + 1], (128, 128)) == sub128
             hot.append(jnp.where(lane, 1.0, 0.0).astype(BF16))
 
-    for copy in copies:
-        copy.wait()
-    added = scatter_faces(returned_rows(back_ref, 6), blocks, lanes)
-    owned = [rows[0:8] + more for rows, more in zip(force + torque, added)]
+    owned = partial
+    for sets in ((0, 1), (2,)):
+        for k in sets:
+            copies[k].wait()
+        added = scatter_sets(back_ref, 6, sets, blocks, lanes)
+        owned = [rows + more for rows, more in zip(owned, added)]
     torque = owned[3:6]
     kept = [jnp.zeros((8, 128), F32) for _ in range(3)]
     columns = []
@@ -614,11 +632,14 @@
         for k in range(3):
             spread_ref[k, 4 * c : 4 * c + 4, :] = rows[8 + 4 * k : 12 + 4 * k]
     spread_ref[:, 12:16, :] = jnp.zeros((3, 4, 128), F32)
-    for copy in send_sets(spread_ref, last_ref, last_send, last_recv, up):
-        copy.wait()
-    added = scatter_faces(returned_rows(last_ref, 3), blocks, lanes)
+    copies = send_sets(spread_ref, last_ref, last_send, last_recv, up)
+    for sets in ((0, 1), (2,)):
+        for k in sets:
+            copies[k].wait()
+        added = scatter_sets(last_ref, 3, sets, blocks, lanes)
+        forces = [rows + more for rows, more in zip(forces, added)]
     for c in range(3):
-        out_ref[8 * c : 8 * c + 8, :] = forces[c] + added[c]
+        out_ref[8 * c : 8 * c + 8, :] = forces[c]
 
 
 def domain_forces(sizes, coords, multipoles, face_atoms, frame_atoms, tile_pairs, tile_count):
@@ -660,7 +681,7 @@
         ]
         + [pltpu.SemaphoreType.DMA((3,))] * 6
         + [pltpu.SemaphoreType.DMA],
-        compiler_params=pltpu.CompilerParams(collective_id=0, has_side_effects=True, vmem_limit_bytes=52 << 20),
+        compiler_params=pltpu.CompilerParams(collective_id=0, has_side_effects=True, vmem_limit_bytes=60 << 20),
     )(coords, multipoles, face_atoms, frame_atoms, tile_pairs, tile_count)
 
 

time: 45.4 us -> 42.5 us (0.936)
  local copies, waits for them, and re-layouts: 3.47 us -> 1.31 us
  Pallas kernels: 40.9 us -> 40.2 us
    unnamed x11 -> x1, local copies, waits for them, and re-layouts: 3.47 us -> 1.31 us
    pallas_call x1, Pallas kernels: 40.9 us -> 40.2 us  [domain_forces(): pl.pallas_call(functools.partial(kernel_body, sizes), out_shape=jax.Shape...]
where the time goes in v5:
time: 42.5 us; the launch traced here: 42.2 us
  Pallas kernels  40.2 us (95%)
  local copies, waits for them, and re-layouts  1.31 us (3%)
  between operations  0.66 us (2%)
    pallas_call x1, Pallas kernels, domain_forces(): pl.pallas_call(functools.partial(kernel_body, sizes), out_shape=jax.Shape...  40.2 us
    unnamed x1, local copies, waits for them, and re-layouts  1.31 us

profile of v5, /device:TPU:1, one launch (start us, length us, event | category | flops | bytes accessed | tf_op | source)
XLA Modules:
  0.0 42.2 jit_solution(242326302926698392)
XLA Ops:
  0.7 40.2 %shard_map.64 = f32[24,128]{1,0:T(8,128)} custom-call(f32[24,128]{1,0:T(8,128)} %bitcast.7, f32[80,128]{1,0:T(8,128)} %bitcast.6, s32[3,4,128]{2,1,0:T(4,128)} %bitcast.9, s32[24,128]{1,0:T(8,128)} %bitcast.8, s32[1,1,2,32]{3,2,1,0:T(2,128)} %pairs_hbm.1, s32[1,1]{1,0:T(1,128)S(6)} %copy.10.count_hbm), custom_call_target="tpu_custom_call" | custom-call | tf_op jit(solution)/shard_map/pallas_call | solution.py:648
  40.9 1.3 %copy.11 = f32[1,1,3,1024]{3,1,2,0:T(1,128)} copy(f32[1,1,3,1024]{3,1,2,0:T(1,128)} %bitcast.5) | data formatting | bytes 24576

commit v6 on v5

--- a/solution.py
+++ b/solution.py
@@ -156,7 +156,7 @@
     return rows
 
 
-def near_rows(f):
+def column_rows(f):
     zero = jnp.zeros_like(f["one"])
     first = [*f["d"], f["dx"], *f["quad"], *f["turned"], f["xqx"], f["one"], *f["x"], *f["xx"]]
     second = [*f["d"], f["dx"], f["q"], *f["qx"], *f["quad"], *f["turned"], f["xqx"], *f["h"]]
@@ -164,14 +164,14 @@
     return first + second + third + [zero] * 7
 
 
-def far_rows(f):
+def coefficient_rows(f):
     zero = jnp.zeros_like(f["one"])
     one = f["one"]
     x, d, q, xx = f["x"], f["d"], f["q"], f["xx"]
     quad, turned = f["quad"], f["turned"]
     z = lambda n: [zero] * n
-    u = [3.0 * x[r] for r in range(3)] + [-3.0 * one] + z(20)
-    v = z(14) + [3.0 * f["dx"]] + [-3.0 * d[r] for r in range(3)] + z(6)
+    u = [-3.0 * x[r] for r in range(3)] + [3.0 * one] + z(20)
+    v = z(14) + [-3.0 * f["dx"]] + [3.0 * d[r] for r in range(3)] + z(6)
     p = z(4) + [15.0 * MULT[e] * xx[e] for e in range(6)] + [-30.0 * x[r] for r in range(3)] + [15.0 * one] + z(10)
     r_ = (
         z(14)
@@ -203,7 +203,7 @@
     return [u, v, p, r_, l1, l2, l3]
 
 
-def far_block(b, sum_scr, far_scr, feat_ref, rhs_ref, place_ref):
+def pool_block(b, sum_scr, col_scr, feat_ref, col_ref, place_ref):
     sums = sum_scr[pl.ds(b, 64, stride=ROWS), :]
     place_ref[b] = sums[8:16]
     hi, lo = split2(sums)
@@ -212,44 +212,41 @@
         parts += [hi[8 * g : 8 * g + 8], lo[8 * g : 8 * g + 8]]
     feat_ref[b] = jnp.concatenate(parts, axis=0).astype(BF16)
     start = 0
+    for group, count in enumerate((24, 24, 40)):
+        rows = col_scr[pl.ds(b + start * ROWS, count, stride=ROWS), :]
+        start += count
+        hi, lo = split2(rows)
+        stacked = jnp.concatenate([hi, hi, lo, jnp.zeros((128 - 3 * count, 128), F32)], axis=0)
+        col_ref[b, group] = stacked.astype(BF16)
+
+
+def own_rows(b, row_scr, row_ref, place_ref, wide_ref):
+    start = 0
     for out_id, count in enumerate((24, 24, 24, 24, 24, 24, 40)):
-        rows = far_scr[pl.ds(b + start * ROWS, count, stride=ROWS), :]
+        rows = row_scr[pl.ds(b + start * 8, count, stride=8), :]
         start += count
         hi, lo = split2(rows)
         pad = [jnp.zeros((128 - 3 * count, 128), F32)]
         stacked = jnp.concatenate([hi, lo, hi] + pad, axis=0).astype(BF16)
-        rhs_ref[b, :, out_id * 128 : (out_id + 1) * 128] = stacked
-
-
-def near_block(b, near_scr, lhs_ref, place_ref, wide_ref):
-    start = 0
-    for group, count in enumerate((24, 24, 40)):
-        rows = near_scr[pl.ds(b + start * 8, count, stride=8), :]
-        start += count
-        hi, lo = split2(rows)
-        stacked = jnp.concatenate([hi, hi, lo, jnp.zeros((128 - 3 * count, 128), F32)], axis=0)
-        lhs_ref[b, :, group * 128 : (group + 1) * 128] = stacked.T.astype(BF16)
+        row_ref[b, out_id * 128 : (out_id + 1) * 128, :] = stacked.T
     place = jnp.concatenate([place_ref[b], jnp.zeros((120, 128), F32)], axis=0).T
     for r in range(3):
         wide_ref[b, r] = jnp.broadcast_to(place[:, r + 1 : r + 2], (128, 128))
 
 
-def store_rows(pool, low, high, sum_scr, far_scr):
+def store_rows(pool, low, high, sum_scr, col_scr):
     f = pool_features([pool[c][low:high] for c in range(13)])
     for n, row in enumerate(sum_rows(f)):
         sum_scr[n * ROWS + low : n * ROWS + high, :] = row
-    at = 0
-    for group in far_rows(f):
-        for row in group:
-            far_scr[at * ROWS + low : at * ROWS + high, :] = row
-            at += 1
+    for n, row in enumerate(column_rows(f)):
+        col_scr[n * ROWS + low : n * ROWS + high, :] = row
     return f
 
 
-def tile_work(near, far, feat_ref, lhs_ref, rhs_ref, place_ref, wide_ref, keep_ref, keep):
-    first = mm(lhs_ref[near, :, 0:128], rhs_ref[far, :, 0:512])
-    second = mm(lhs_ref[near, :, 128:256], rhs_ref[far, :, 512:768])
-    third = mm(lhs_ref[near, :, 256:384], rhs_ref[far, :, 768:896])
+def tile_work(near, far, row_ref, col_ref, place_ref, wide_ref, keep_ref, keep):
+    first = mm(row_ref[near, 0:512, :], col_ref[far, 0])
+    second = mm(row_ref[near, 512:768, :], col_ref[far, 1])
+    third = mm(row_ref[near, 768:896, :], col_ref[far, 2])
     chunk = 32
     names = ("b1", "b2", "b3", "al", "be", "ga", "de", "e1")
     pieces = {name: ([], []) for name in names}
@@ -264,9 +261,10 @@
         b1 = b0 * t
         b2 = b1 * t
         b3 = b2 * t
-        u, v = first[rows, 0:128], first[rows, 128:256]
-        pt, rt = first[rows, 256:384] * t, first[rows, 384:512] * t
-        l1, l2, l3 = second[rows, 0:128], second[rows, 128:256], third[rows, :]
+        v, u, r_, p = [first[n * 128 + row : n * 128 + row + chunk] for n in range(4)]
+        rt, pt = r_ * t, p * t
+        l1, l2 = [second[n * 128 + row : n * 128 + row + chunk] for n in range(2)]
+        l3 = third[rows]
         gr, gp = 1.4 * rt - v, 1.4 * pt + u
         al = b2 * (rt - v)
         be = b2 * (pt + u)
@@ -470,7 +468,7 @@
 def kernel_body(
     sizes, coords_hbm, mult_hbm, face_hbm, frame_hbm, pairs_hbm, count_hbm, out_ref,
     coords_ref, mult_ref, face_ref, frame_ref, pairs_ref, count_ref, load_sem, send_ref, import_ref, halo_ref, back_ref, spread_ref, last_ref, table_ref, smem_ref,
-    pool_ref, sum_scr, near_scr, far_scr, feat_ref, lhs_ref, rhs_ref, place_ref, wide_ref, keep_ref, runs_ref, acc_ref,
+    pool_ref, sum_scr, row_scr, col_scr, feat_ref, row_ref, col_ref, place_ref, wide_ref, keep_ref, runs_ref, acc_ref,
     send_sem, recv_sem, back_send, back_recv, last_send, last_recv, local_sem,
 ):
     up, down = neighbours(sizes)
@@ -503,9 +501,9 @@
     for c in range(13):
         pool_ref[c, 0:8, :] = own[c]
         pool_ref[c, 20:24, :] = jnp.zeros((4, 128), F32)
-    f = store_rows(own, 0, 8, sum_scr, far_scr)
-    for n, row in enumerate(near_rows(f)):
-        near_scr[n * 8 : n * 8 + 8, :] = row
+    f = store_rows(own, 0, 8, sum_scr, col_scr)
+    for n, row in enumerate([row for group in coefficient_rows(f) for row in group]):
+        row_scr[n * 8 : n * 8 + 8, :] = row
     above = lax.broadcasted_iota(jnp.int32, (128, 128), 0) < lax.broadcasted_iota(jnp.int32, (128, 128), 1)
     keep_ref[0] = jnp.ones((128, 128), F32)
     keep_ref[1] = jnp.where(above, 1.0, 0.0).astype(F32)
@@ -515,15 +513,15 @@
         acc_ref[b * 8 * ACC_GROUPS : (b + 1) * 8 * ACC_GROUPS, :] = jnp.zeros((8 * ACC_GROUPS, 128), F32)
 
     def own_block(b, _):
-        far_block(b, sum_scr, far_scr, feat_ref, rhs_ref, place_ref)
-        near_block(b, near_scr, lhs_ref, place_ref, wide_ref)
+        pool_block(b, sum_scr, col_scr, feat_ref, col_ref, place_ref)
+        own_rows(b, row_scr, row_ref, place_ref, wide_ref)
         return 0
 
     lax.fori_loop(0, OWN_BLOCKS, own_block, 0, unroll=4)
     table_copy.wait()
 
     def import_block(b, _):
-        far_block(b, sum_scr, far_scr, feat_ref, rhs_ref, place_ref)
+        pool_block(b, sum_scr, col_scr, feat_ref, col_ref, place_ref)
         return 0
 
     for sets, rows, blocks in (((0, 1), (8, 16), (8, 16)), ((2,), (16, 24), (16, 20))):
@@ -532,13 +530,13 @@
         for c in range(13):
             for k in sets:
                 pool_ref[c, 8 + 4 * k : 12 + 4 * k, :] = import_ref[k, 4 * c : 4 * c + 4, :]
-        store_rows([pool_ref[c] for c in range(13)], *rows, sum_scr, far_scr)
+        store_rows([pool_ref[c] for c in range(13)], *rows, sum_scr, col_scr)
         lax.fori_loop(*blocks, import_block, 0, unroll=4)
 
     def one(t):
         near, far = pairs_ref[0, 0, 0, t], pairs_ref[0, 0, 1, t]
         keep = jnp.where(t < count_ref[0, 0], jnp.where(near == far, 1, 0), 2)
-        return t, near, far, tile_work(near, far, feat_ref, lhs_ref, rhs_ref, place_ref, wide_ref, keep_ref, keep)
+        return t, near, far, tile_work(near, far, row_ref, col_ref, place_ref, wide_ref, keep_ref, keep)
 
     def sums(t, near, far, w):
         before = [smem_ref[0, 2 * t + side] for side in range(2)]
@@ -668,11 +666,11 @@
             pltpu.SMEM((8, 128), jnp.int32),
             pltpu.VMEM((13, ROWS, 128), F32),
             pltpu.VMEM((64 * ROWS, 128), F32),
-            pltpu.VMEM((88 * 8, 128), F32),
-            pltpu.VMEM((184 * ROWS, 128), F32),
+            pltpu.VMEM((184 * 8, 128), F32),
+            pltpu.VMEM((88 * ROWS, 128), F32),
             pltpu.VMEM((POOL_BLOCKS, 128, 128), BF16),
-            pltpu.VMEM((OWN_BLOCKS, 128, 384), BF16),
-            pltpu.VMEM((POOL_BLOCKS, 128, 896), BF16),
+            pltpu.VMEM((OWN_BLOCKS, 896, 128), BF16),
+            pltpu.VMEM((POOL_BLOCKS, 3, 128, 128), BF16),
             pltpu.VMEM((POOL_BLOCKS, 8, 128), F32),
             pltpu.VMEM((OWN_BLOCKS, 3, 128, 128), F32),
             pltpu.VMEM((3, 128, 128), F32),
@@ -681,8 +679,8 @@
         ]
         + [pltpu.SemaphoreType.DMA((3,))] * 6
         + [pltpu.SemaphoreType.DMA],
-        compiler_params=pltpu.CompilerParams(collective_id=0, has_side_effects=True, vmem_limit_bytes=60 << 20),
-    )(coords, multipoles, face_atoms, frame_atoms, tile_pairs, tile_count)
+        compiler_params=pltpu.CompilerParams(collective_id=0, has_side_effects=True, vmem_limit_bytes=52 << 20),
+    )(*[pltpu.with_memory_space_constraint(a, pltpu.HBM) for a in (coords, multipoles, face_atoms, frame_atoms, tile_pairs)], tile_count)
 
 
 def solution(mesh):

time: 42.5 us -> 40.6 us (0.955)
  Pallas kernels: 40.2 us -> 39.2 us
  local copies, waits for them, and re-layouts: 1.31 us -> 0.6 us
    pallas_call x1, Pallas kernels: 40.2 us -> 39.2 us  [domain_forces(): pl.pallas_call(functools.partial(kernel_body, sizes), out_shape=jax.Shape...]
    unnamed x1, local copies, waits for them, and re-layouts: 1.31 us -> 0.6 us
where the time goes in v6:
time: 40.6 us; the launch traced here: 40.4 us
  Pallas kernels  39.2 us (97%)
  between operations  0.66 us (2%)
  local copies, waits for them, and re-layouts  0.6 us (1%)
    pallas_call x1, Pallas kernels, domain_forces(): pl.pallas_call(functools.partial(kernel_body, sizes), out_shape=jax.Shape...  39.2 us

profile of v6, /device:TPU:1, one launch (start us, length us, event | category | flops | bytes accessed | tf_op | source)
XLA Modules:
  0.0 40.4 jit_solution(11993818343386557019)
XLA Ops:
  0.7 39.2 %shard_map.64 = f32[24,128]{1,0:T(8,128)S(1)} custom-call(f32[24,128]{1,0:T(8,128)} %bitcast.7, f32[80,128]{1,0:T(8,128)} %bitcast.6, s32[3,4,128]{2,1,0:T(4,128)} %bitcast.9, s32[24,128]{1,0:T(8,128)} %bitcast.8, s32[1,1,2,32]{3,2,1,0:T(2,128)} %pairs_hbm.1, s32[1,1]{1,0:T(1,128)S(6)} %copy.10.count_hbm), custom_call_target="tpu_custom_call" | custom-call | tf_op jit(solution)/shard_map/pallas_call | solution.py:646
  39.8 0.6 %copy.11 = f32[1,1,3,1024]{3,1,2,0:T(1,128)} copy(f32[1,1,3,1024]{3,1,2,0:T(1,128)S(1)} %bitcast.5) | data formatting | bytes 24576

commit v7 on v6

--- a/solution.py
+++ b/solution.py
@@ -19,7 +19,7 @@
 BF16 = jnp.bfloat16
 ACC_GROUPS = 18
 EVENTS = 64
-TILE_STEP = 16
+TILE_STEP = 32
 MESH = pl.DeviceIdType.MESH
 
 
@@ -111,19 +111,19 @@
         pl.semaphore_signal(pltpu.get_barrier_semaphore(), inc=1, device_id=peer, device_id_type=MESH)
 
 
-def send_sets(send_ref, recv_ref, send_sem, recv_sem, targets):
-    copies = []
-    for k, peer in enumerate(targets):
+def send_sets(send_ref, recv_ref, send_sem, recv_sem, targets, sets=(2, 0, 1)):
+    copies = {}
+    for k in sets:
         copy = pltpu.make_async_remote_copy(
             src_ref=send_ref.at[k],
             dst_ref=recv_ref.at[k],
             send_sem=send_sem.at[k],
             recv_sem=recv_sem.at[k],
-            device_id=peer,
+            device_id=targets[k],
             device_id_type=MESH,
         )
         copy.start()
-        copies.append(copy)
+        copies[k] = copy
     return copies
 
 
@@ -488,12 +488,14 @@
     ]
     for copy in loads:
         copy.start()
-    for copy in loads:
+    for copy in loads[:3]:
         copy.wait()
     gather_exports(coords_ref, mult_ref, face_ref, send_ref)
     pl.semaphore_wait(pltpu.get_barrier_semaphore(), 3)
     copies = send_sets(send_ref, import_ref, send_sem, recv_sem, down)
 
+    for copy in loads[3:]:
+        copy.wait()
     event_tables(pairs_ref, table_ref)
     table_copy = pltpu.make_async_copy(table_ref, smem_ref, local_sem)
     table_copy.start()
@@ -572,10 +574,12 @@
         force, torque = finish_sums(load, pool_features([pool_ref[c, low:high, :] for c in range(13)]))
         return force + torque
 
-    for c, rows in enumerate(finish(8, 24)):
-        for k in range(3):
-            halo_ref[k, 4 * c : 4 * c + 4, :] = rows[4 * k : 4 * k + 4]
-    copies = send_sets(halo_ref, back_ref, back_send, back_recv, up)
+    copies = {}
+    for sets, low in (((2,), 16), ((0, 1), 8)):
+        for c, rows in enumerate(finish(low, low + 8)):
+            for n, k in enumerate(sets):
+                halo_ref[k, 4 * c : 4 * c + 4, :] = rows[4 * n : 4 * n + 4]
+        copies.update(send_sets(halo_ref, back_ref, back_send, back_recv, up, sets))
     partial = finish(0, 8)
 
     blocks, lanes = face_masks([face_ref[k, j : j + 1, :] for k in range(3) for j in range(4)])

time: 40.6 us -> 40 us (0.985)
  Pallas kernels: 39.2 us -> 38.6 us
    pallas_call x1, Pallas kernels: 39.2 us -> 38.6 us  [domain_forces(): pl.pallas_call(functools.partial(kernel_body, sizes), out_shape=jax.Shape...]
where the time goes in v7:
time: 40 us; the launch traced here: 39.9 us
  Pallas kernels  38.6 us (96%)
  between operations  0.66 us (2%)
  local copies, waits for them, and re-layouts  0.6 us (2%)
    pallas_call x1, Pallas kernels, domain_forces(): pl.pallas_call(functools.partial(kernel_body, sizes), out_shape=jax.Shape...  38.6 us

profile of v7, /device:TPU:1, one launch (start us, length us, event | category | flops | bytes accessed | tf_op | source)
XLA Modules:
  0.0 39.9 jit_solution(3312868243318339392)
XLA Ops:
  0.7 38.6 %shard_map.64 = f32[24,128]{1,0:T(8,128)S(1)} custom-call(f32[24,128]{1,0:T(8,128)} %bitcast.7, f32[80,128]{1,0:T(8,128)} %bitcast.6, s32[3,4,128]{2,1,0:T(4,128)} %bitcast.9, s32[24,128]{1,0:T(8,128)} %bitcast.8, s32[1,1,2,32]{3,2,1,0:T(2,128)} %pairs_hbm.1, s32[1,1]{1,0:T(1,128)S(6)} %copy.10.count_hbm), custom_call_target="tpu_custom_call" | custom-call | tf_op jit(solution)/shard_map/pallas_call | solution.py:650
  39.3 0.6 %copy.11 = f32[1,1,3,1024]{3,1,2,0:T(1,128)} copy(f32[1,1,3,1024]{3,1,2,0:T(1,128)S(1)} %bitcast.5) | data formatting | bytes 24576

commit v8 on v7

--- a/solution.py
+++ b/solution.py
@@ -519,7 +519,7 @@
         own_rows(b, row_scr, row_ref, place_ref, wide_ref)
         return 0
 
-    lax.fori_loop(0, OWN_BLOCKS, own_block, 0, unroll=4)
+    lax.fori_loop(0, OWN_BLOCKS, own_block, 0, unroll=8)
     table_copy.wait()
 
     def import_block(b, _):
@@ -533,7 +533,7 @@
             for k in sets:
                 pool_ref[c, 8 + 4 * k : 12 + 4 * k, :] = import_ref[k, 4 * c : 4 * c + 4, :]
         store_rows([pool_ref[c] for c in range(13)], *rows, sum_scr, col_scr)
-        lax.fori_loop(*blocks, import_block, 0, unroll=4)
+        lax.fori_loop(*blocks, import_block, 0, unroll=blocks[1] - blocks[0])
 
     def one(t):
         near, far = pairs_ref[0, 0, 0, t], pairs_ref[0, 0, 1, t]

time: 40 us -> 40 us (level)
  no operation moved by 1% of the time
where the time goes in v8:
time: 40 us; the launch traced here: 39.9 us
  Pallas kernels  38.6 us (96%)
  between operations  0.66 us (2%)
  local copies, waits for them, and re-layouts  0.6 us (2%)
    pallas_call x1, Pallas kernels, domain_forces(): pl.pallas_call(functools.partial(kernel_body, sizes), out_shape=jax.Shape...  38.6 us

profile of v8, /device:TPU:1, one launch (start us, length us, event | category | flops | bytes accessed | tf_op | source)
XLA Modules:
  0.0 39.9 jit_solution(6972321737451047034)
XLA Ops:
  0.7 38.6 %shard_map.64 = f32[24,128]{1,0:T(8,128)S(1)} custom-call(f32[24,128]{1,0:T(8,128)} %bitcast.7, f32[80,128]{1,0:T(8,128)} %bitcast.6, s32[3,4,128]{2,1,0:T(4,128)} %bitcast.9, s32[24,128]{1,0:T(8,128)} %bitcast.8, s32[1,1,2,32]{3,2,1,0:T(2,128)} %pairs_hbm.1, s32[1,1]{1,0:T(1,128)S(6)} %copy.10.count_hbm), custom_call_target="tpu_custom_call" | custom-call | tf_op jit(solution)/shard_map/pallas_call | solution.py:650
  39.3 0.6 %copy.11 = f32[1,1,3,1024]{3,1,2,0:T(1,128)} copy(f32[1,1,3,1024]{3,1,2,0:T(1,128)S(1)} %bitcast.5) | data formatting | bytes 24576
